TPU v7x, 32 devices: a whole 2x2x4 slice. The times are simulated.
32 devices in a mesh: lat: 16 (over z, y, x), field: 2 (over core).
Axes of the slice: x: 2, y: 2, z: 4, core: 2. Of those that a mesh axis runs over, the one named last changes fastest.
Arguments:
- precip: float32 [4, 512, 1024], P('field', 'lat'), as said below
Outputs:
- barycenter: float32 [512, 1024], P('lat')
- scaling_logs: float32 [4, 512, 1024], P('field', 'lat')
Inputs may be any that keep to these rules, and one draw needn't show every extreme that they name: `precip`: Nonnegative; each cell is dry (zero) or wet independently of the others.
All inputs are finite; a program needn't handle non-finite values.
Results may differ from a plain program's by a relative error of at most 0.0012.
Values sent between devices are 32-bit elements; how exact they have to be, the bound alone decides.
No kernel may reach another device: no remote copies, remote signals or barrier semaphores. Data moves between devices by JAX's collectives and lax.ppermute only.
A program may use at most 128 MiB of HBM per device.

v0:
```python
import math

import jax
import jax.numpy as jnp
import ml_dtypes
import numpy as np
from jax import lax
from jax.experimental import pallas as pl
from jax.experimental.pallas import tpu as pltpu
from jax.sharding import PartitionSpec as P

ITERS = 2


heat_rate = 2.0
floor_value = 0.1


def colatitudes(lat_total):
    index_rows = jnp.arange(lat_total, dtype=jnp.float32)
    return jnp.pi * (index_rows + 0.5) / lat_total


def quad_weights(lat_total, lon_total):
    polar_angle = colatitudes(lat_total)
    return jnp.sin(polar_angle) * (jnp.pi / lat_total) * (2.0 * jnp.pi / lon_total)


def heat_factors(degrees):
    level = jnp.arange(degrees, dtype=jnp.float32)
    return jnp.exp(-heat_rate * level * (level + 1.0) / (degrees * (degrees - 1.0)))


def legendre_north(orders, lat_total, degrees):
    half_rows = lat_total // 2
    polar_angle = colatitudes(lat_total)[:half_rows]
    cosine = jnp.cos(polar_angle)
    log_sine = jnp.log(jnp.sin(polar_angle))
    order_value = orders.astype(jnp.float32)
    step_count = jnp.arange(1, degrees + 1, dtype=jnp.float32)
    log_ratios = jnp.log((2.0 * step_count - 1.0) / (2.0 * step_count))
    within = step_count[None, :] <= order_value[:, None]
    partial_log = jnp.sum(jnp.where(within, log_ratios[None, :], 0.0), axis=1)
    log_start = 0.5 * jnp.log((2.0 * order_value + 1.0) / (4.0 * jnp.pi)) + 0.5 * partial_log
    start_log = log_start[:, None] + order_value[:, None] * log_sine[None, :]
    span_size = min(32, degrees)

    def advance(state, block_start):
        prev_one, prev_two, log_scale = state
        collected = []
        for offset in range(span_size):
            degree = (block_start + offset).astype(jnp.float32)
            safe_diff = jnp.maximum(degree * degree - order_value * order_value, 1.0)
            first_factor = jnp.sqrt((4.0 * degree * degree - 1.0) / safe_diff)
            numerator = (
                (2.0 * degree + 1.0) * (degree + order_value - 1.0) * (degree - order_value - 1.0)
            )
            denominator = jnp.maximum((2.0 * degree - 3.0) * safe_diff, 1.0)
            second_factor = jnp.sqrt(jnp.maximum(numerator, 0.0) / denominator)
            recurred = (
                first_factor[:, None] * cosine[None, :] * prev_one
                - second_factor[:, None] * prev_two
            )
            current = jnp.where(
                (degree > order_value)[:, None],
                recurred,
                jnp.where(
                    (degree == order_value)[:, None],
                    jnp.ones_like(recurred),
                    jnp.zeros_like(recurred),
                ),
            )
            collected.append(current * jnp.exp(log_scale))
            prev_two = prev_one
            prev_one = current
            if (offset + 1) % 8 == 0:
                magnitude = jnp.maximum(jnp.abs(prev_one), jnp.abs(prev_two))
                safe_size = jnp.where(magnitude > 0.0, magnitude, jnp.ones_like(magnitude))
                prev_one = prev_one / safe_size
                prev_two = prev_two / safe_size
                log_scale = log_scale + jnp.log(safe_size)
        return ((prev_one, prev_two, log_scale), jnp.stack(collected))

    empty_state = jnp.zeros((orders.shape[0], half_rows), jnp.float32)
    block_starts = jnp.arange(0, degrees, span_size, dtype=jnp.int32)
    final_state, stacked = lax.scan(advance, (empty_state, empty_state, start_log), block_starts)
    legendre = stacked.reshape(degrees, orders.shape[0], half_rows)
    return jnp.transpose(legendre, (1, 2, 0))


def fourier_tables(lon_total, degrees, groups):
    per_group = degrees // groups
    column = jnp.arange(2 * degrees, dtype=jnp.int32)
    group_index = column // (2 * per_group)
    within_group = column % (2 * per_group)
    part_index = within_group // per_group
    order_index = group_index * per_group + within_group % per_group
    points = jnp.arange(lon_total, dtype=jnp.int32)
    phase = (points[:, None] * order_index[None, :] % lon_total).astype(jnp.float32) * (
        2.0 * jnp.pi / lon_total
    )
    forward = jnp.where(part_index[None, :] == 0, jnp.cos(phase), -jnp.sin(phase))
    doubled = jnp.where(order_index == 0, 1.0, 2.0)
    backward = jnp.transpose(forward) * doubled[:, None]
    return (forward, backward)


def on_device_plain(precip):
    groups = lax.axis_size("lat")
    lat_index = lax.axis_index("lat")
    local_fields, lat_rows, lon_total = precip.shape
    lat_total = lat_rows * groups
    degrees = lon_total // 2
    orders_here = degrees // groups
    half_rows = lat_total // 2
    count_fields = local_fields * lax.axis_size("field")
    weights_all = quad_weights(lat_total, lon_total)
    local_weights = lax.dynamic_slice_in_dim(weights_all, lat_index * lat_rows, lat_rows)
    forward, backward = fourier_tables(lon_total, degrees, groups)
    heat_factor = heat_factors(degrees)
    orders = lat_index * orders_here + jnp.arange(orders_here, dtype=jnp.int32)
    north_table = legendre_north(orders, lat_total, degrees)
    paired = north_table.reshape(orders_here, half_rows, degrees // 2, 2)
    parity = (orders % 2 == 0)[:, None, None]
    even_table = jnp.where(parity, paired[..., 0], paired[..., 1])
    odd_table = jnp.where(parity, paired[..., 1], paired[..., 0])
    heat_paired = heat_factor.reshape(degrees // 2, 2)
    heat_even = jnp.where(parity[:, :, 0], heat_paired[None, :, 0], heat_paired[None, :, 1])
    heat_odd = jnp.where(parity[:, :, 0], heat_paired[None, :, 1], heat_paired[None, :, 0])
    weights_north = weights_all[:half_rows]

    def legendre_pass(spread):
        count_here = spread.shape[0]
        shaped = spread.reshape(count_here, lat_total, 2, orders_here)
        north_part = shaped[:, :half_rows]
        south_part = jnp.flip(shaped[:, half_rows:], axis=1)
        even_input = (north_part + south_part) * weights_north[None, :, None, None]
        odd_input = (north_part - south_part) * weights_north[None, :, None, None]
        even_coef = jnp.einsum(
            "mjk,fjpm->mfpk", even_table, even_input, precision=lax.Precision.HIGHEST
        )
        odd_coef = jnp.einsum(
            "mjk,fjpm->mfpk", odd_table, odd_input, precision=lax.Precision.HIGHEST
        )
        even_coef = even_coef * heat_even[:, None, None, :]
        odd_coef = odd_coef * heat_odd[:, None, None, :]
        even_sum = jnp.einsum(
            "mjk,mfpk->fjpm", even_table, even_coef, precision=lax.Precision.HIGHEST
        )
        odd_sum = jnp.einsum("mjk,mfpk->fjpm", odd_table, odd_coef, precision=lax.Precision.HIGHEST)
        result = jnp.concatenate([even_sum + odd_sum, jnp.flip(even_sum - odd_sum, axis=1)], axis=1)
        return result.reshape(count_here, lat_total, 2 * orders_here)

    def kernel_apply_step(fields):
        spectra = jnp.einsum("fjk,kc->fjc", fields, forward, precision=lax.Precision.HIGHEST)

        def one_member(carry, member_spectra):
            spread = lax.all_to_all(member_spectra, "lat", split_axis=1, concat_axis=0, tiled=True)
            filtered = legendre_pass(spread[None])
            returned = lax.all_to_all(filtered[0], "lat", split_axis=0, concat_axis=1, tiled=True)
            return (carry, returned)

        unused, gathered = lax.scan(one_member, jnp.zeros((), jnp.float32), spectra)
        return jnp.einsum("fjc,ck->fjk", gathered, backward, precision=lax.Precision.HIGHEST)

    partial_value = jnp.sum(precip * local_weights[None, :, None], axis=(1, 2))
    masses = lax.psum(partial_value, "lat") / (4.0 * jnp.pi)
    scaling_logs = jnp.zeros(precip.shape, jnp.float32)
    log_barycenter = jnp.zeros(precip.shape[1:], jnp.float32)
    scaled = precip / masses[:, None, None]
    ratio_field = scaled
    for sweep in range(ITERS):
        smoothed = kernel_apply_step(ratio_field)
        clamped_values = jnp.log(jnp.maximum(smoothed, floor_value))
        added_total = lax.psum(jnp.sum(scaling_logs + clamped_values, axis=0), "field")
        log_barycenter = added_total / count_fields
        scaling_logs = log_barycenter[None] - clamped_values
        if sweep + 1 < ITERS:
            blurred_scale = kernel_apply_step(jnp.exp(scaling_logs))
            ratio_field = scaled / jnp.maximum(blurred_scale, floor_value)
    return (jnp.exp(log_barycenter), scaling_logs)


QUART = 4


def split_pair(value):
    high = value.astype(jnp.bfloat16)
    low = (value - high.astype(jnp.float32)).astype(jnp.bfloat16)
    return high, low


def pair_rows(value):
    high, low = split_pair(value)
    return jnp.concatenate([high, low], axis=0)


def dot_nt(left, right):
    return lax.dot_general(left, right, (((1,), (1,)), ((), ())), preferred_element_type=jnp.float32)


def dot_nn(left, right):
    return lax.dot_general(left, right, (((1,), (0,)), ((), ())), preferred_element_type=jnp.float32)


def wave_tables(lon_total, devices, slots):
    span = lon_total // QUART
    residue = np.arange(QUART)[:, None, None]
    order = residue + QUART * np.arange(devices // QUART)[None, :, None]
    order = (order + devices * np.arange(slots)[None, None, :]).reshape(QUART, -1)
    phase = (order[:, :, None] * np.arange(span)[None, None, :] % lon_total) * (2.0 * np.pi / lon_total)
    table = np.concatenate([np.cos(phase), np.sin(phase)], axis=1).astype(np.float32)
    high = table.astype(ml_dtypes.bfloat16)
    low = (table - high.astype(np.float32)).astype(ml_dtypes.bfloat16)
    return high, low


def forward_waves(field, high_ref, low_ref, out_ref):
    span = field.shape[1] // QUART
    rows = field.shape[0]
    lanes = 2 * rows
    part = [field[:, q * span : (q + 1) * span] for q in range(QUART)]
    sum_even, sum_odd = part[0] + part[2], part[1] + part[3]
    diff_even, diff_odd = part[0] - part[2], part[1] - part[3]
    stack_even = pair_rows(jnp.concatenate([sum_even + sum_odd, sum_even - sum_odd], axis=0))
    stack_odd = pair_rows(jnp.concatenate([diff_even, diff_odd], axis=0))
    orders = high_ref.shape[1] // 2
    first = lax.broadcasted_iota(jnp.int32, (orders, lanes), 1) < rows
    for residue in range(QUART):
        stack = stack_odd if residue % 2 else stack_even
        found = dot_nt(high_ref[residue], stack) + dot_nt(low_ref[residue], stack)
        found = found[:, :lanes] + found[:, lanes:]
        cosine, sine = found[:orders], found[orders:]
        if residue == 0:
            packed = jnp.where(first, cosine, -pltpu.roll(sine, rows, 1))
        elif residue == 2:
            packed = jnp.where(first, pltpu.roll(cosine, rows, 1), -sine)
        elif residue == 1:
            packed = jnp.where(first, cosine, -cosine) - pltpu.roll(sine, rows, 1)
        else:
            turned = pltpu.roll(sine, rows, 1)
            packed = cosine + jnp.where(first, turned, -turned)
        out_ref[:, residue] = packed.reshape(out_ref.shape[0], out_ref.shape[2], lanes)


def inverse_waves(spec_ref, high_ref, low_ref):
    outer, _, slots, lanes = spec_ref.shape
    rows = lanes // 2
    real = [None] * QUART
    cross = {}
    spare = None
    for residue in range(QUART):
        turned = jnp.transpose(spec_ref[:, residue].reshape(outer * slots, lanes))
        cosine, sine = turned[:rows], turned[rows:]
        if residue == 0:
            spare = sine[:, 0:1]
        left = jnp.concatenate([cosine, -sine], axis=1)
        if residue % 2:
            left = jnp.concatenate([left, jnp.concatenate([sine, cosine], axis=1)], axis=0)
        count = left.shape[0]
        left = pair_rows(left)
        found = dot_nn(left, high_ref[residue]) + dot_nn(left, low_ref[residue])
        found = found[:count] + found[count:]
        real[residue] = found[:rows]
        if residue % 2:
            cross[residue] = found[rows:]
    plus, minus = real[0] + real[2], real[0] - real[2]
    both, gap = real[1] + real[3], cross[1] - cross[3]
    return jnp.concatenate([plus + both, minus - gap, plus - both, minus + gap], axis=1), spare


def copy_flipped(src_ref, dst_ref, south, lat_rows):
    rows = src_ref.shape[0]
    for row in range(rows):
        base, offset = row - row % lat_rows, row % lat_rows
        target = base + jnp.where(south, lat_rows - 1 - offset, offset)
        dst_ref[pl.ds(target, 1), :] = src_ref[row : row + 1, :]


def first_body(lat_rows, dev_ref, field_ref, high_ref, low_ref, flipped_ref, out_ref):
    copy_flipped(field_ref, flipped_ref, dev_ref[1] > 0, lat_rows)
    forward_waves(flipped_ref[...], high_ref, low_ref, out_ref)


def member_sum(value, lat_rows):
    total = value[:lat_rows]
    for member in range(1, value.shape[0] // lat_rows):
        total = total + value[member * lat_rows : (member + 1) * lat_rows]
    return total


def mass_body(lat_rows, spec_ref, field_ref, high_ref, low_ref, clamp_ref, sum_ref, scaled_ref):
    blurred, total = inverse_waves(spec_ref, high_ref, low_ref)
    inverse = (4.0 * math.pi) / total
    scaled_ref[...] = field_ref[...] * inverse
    clamped = jnp.log(jnp.maximum(blurred * inverse, floor_value))
    clamp_ref[...] = clamped
    sum_ref[...] = member_sum(clamped, lat_rows)


def center_body(count, lat_rows, clamp_ref, sum_ref, other_ref, high_ref, low_ref, logs_ref, out_ref):
    center = (sum_ref[...] + other_ref[...]) / count
    members = clamp_ref.shape[0] // lat_rows
    logs = jnp.concatenate([center] * members, axis=0) - clamp_ref[...]
    logs_ref[...] = logs
    forward_waves(jnp.exp(logs), high_ref, low_ref, out_ref)


def ratio_body(spec_ref, scaled_ref, high_ref, low_ref, out_ref):
    blurred, _ = inverse_waves(spec_ref, high_ref, low_ref)
    forward_waves(scaled_ref[...] / jnp.maximum(blurred, floor_value), high_ref, low_ref, out_ref)


def last_body(lat_rows, dev_ref, spec_ref, logs_ref, high_ref, low_ref, clamp_ref, sum_ref, clamp_tmp, sum_tmp):
    blurred, _ = inverse_waves(spec_ref, high_ref, low_ref)
    clamped = jnp.log(jnp.maximum(blurred, floor_value))
    clamp_tmp[...] = clamped
    sum_tmp[...] = member_sum(logs_ref[...] + clamped, lat_rows)
    copy_flipped(clamp_tmp, clamp_ref, dev_ref[1] > 0, lat_rows)
    copy_flipped(sum_tmp, sum_ref, dev_ref[1] > 0, lat_rows)


def table_rows(degrees, devices, slot):
    return (degrees - devices * slot) // 2


def table_offset(degrees, devices, slot, parity):
    start = sum(2 * table_rows(degrees, devices, s) for s in range(slot))
    return start + parity * table_rows(degrees, devices, slot)


def legendre_body(degrees, devices, slots, dev_ref, place_ref, start_ref, high_ref, low_ref,
                  first_coef, second_coef, left_half, right_half):
    half = (left_half, right_half)
    lanes = 128
    device = dev_ref[0]
    order = lax.broadcasted_iota(jnp.int32, (slots, degrees), 0) * devices + device
    level = lax.broadcasted_iota(jnp.int32, (slots, degrees), 1)
    above = level > order
    order, level = order.astype(jnp.float32), level.astype(jnp.float32)
    diff = jnp.maximum(level * level - order * order, 1.0)
    first_coef[...] = jnp.where(above, jnp.sqrt((4.0 * level * level - 1.0) / diff), 0.0)
    numer = (2.0 * level + 1.0) * (level + order - 1.0) * (level - order - 1.0)
    denom = jnp.maximum((2.0 * level - 3.0) * diff, 1.0)
    second_coef[...] = jnp.where(above, jnp.sqrt(jnp.maximum(numer, 0.0) / denom), 0.0)

    lane = lax.broadcasted_iota(jnp.int32, (slots, lanes), 1)
    start = jnp.sum(jnp.where(lane == device, start_ref[...], 0.0), axis=1, keepdims=True)
    sub = lax.broadcasted_iota(jnp.int32, (8, lanes), 0)
    tiles = slots // 8
    cosine = [jnp.broadcast_to(place_ref[0:1, h * lanes : (h + 1) * lanes], (8, lanes)) for h in range(2)]
    log_sine = [jnp.broadcast_to(place_ref[1:2, h * lanes : (h + 1) * lanes], (8, lanes)) for h in range(2)]
    order_tile = [(sub + 8 * t) * devices + device for t in range(tiles)]
    zero = jnp.zeros((8, lanes), jnp.float32)
    span_log = 60.0 * math.log(2.0)

    def fresh(tile):
        state = []
        for h in range(2):
            scale_log = start[8 * tile : 8 * tile + 8] + order_tile[tile].astype(jnp.float32) * log_sine[h]
            state.append((zero, zero, scale_log, jnp.exp(scale_log)))
        return state

    def chunk(index, states):
        active = len(states)
        base = pl.multiple_of(index * lanes, lanes)
        first = [first_coef[8 * t : 8 * t + 8, pl.ds(base, lanes)] for t in range(active)]
        second = [second_coef[8 * t : 8 * t + 8, pl.ds(base, lanes)] for t in range(active)]
        states = [list(s) for s in states]
        for k in range(lanes):
            degree = base + k
            for t in range(active):
                a = jnp.broadcast_to(first[t][:, k : k + 1], (8, lanes))
                b = jnp.broadcast_to(second[t][:, k : k + 1], (8, lanes))
                begin = jnp.where(order_tile[t] == degree, 1.0, 0.0)
                for h in range(2):
                    one, two, scale_log, scale = states[t][h]
                    now = (a * cosine[h]) * one + (begin - b * two)
                    half[h][pl.ds(degree * slots + 8 * t, 8), :] = now * scale
                    two, one = one, now
                    if (k + 1) % 8 == 0:
                        large = jnp.maximum(jnp.abs(one), jnp.abs(two)) > 2.0**30
                        factor = jnp.where(large, 2.0**-60, 1.0)
                        one, two = one * factor, two * factor
                        scale_log = scale_log + jnp.where(large, span_log, 0.0)
                        scale = jnp.exp(scale_log)
                    states[t][h] = (one, two, scale_log, scale)
        return states

    states = []
    chunks = degrees // lanes
    for index in range(chunks):
        while len(states) < tiles and 8 * len(states) * devices < (index + 1) * lanes:
            states.append(fresh(len(states)))
        states = chunk(index, states)

    for slot in range(slots):
        count = table_rows(degrees, devices, slot)
        for parity in range(2):
            offset = table_offset(degrees, devices, slot, parity)
            begin = (devices * slot + parity) * slots + slot
            for h in range(2):
                high, low = split_pair(half[h][pl.ds(begin, count, stride=2 * slots), :])
                high_ref[offset : offset + count, h * lanes : (h + 1) * lanes] = high
                low_ref[offset : offset + count, h * lanes : (h + 1) * lanes] = low


def sphere_body(degrees, devices, slots, lat_groups, lat_rows, members, with_mass, dev_ref, spec_ref, high_ref,
                low_ref, weight_ref, heat_ref, out_ref, even_in0, even_in1, odd_in0, odd_in1,
                north0, north1, south0, south1):
    device = dev_ref[0]
    sign = jnp.where(device % 2 == 0, 1.0, -1.0)
    fields = devices // lat_groups
    half_groups = lat_groups // 2
    per_field = 2 * members
    columns = fields * per_field
    group_lanes = 128 // lat_rows
    for field in range(fields):
        for h in range(2):
            even, odd = [], []
            for q in range(group_lanes):
                lat = h * group_lanes + q
                north = spec_ref[lat * fields + field]
                south = spec_ref[(lat_groups - 1 - lat) * fields + field] * sign
                even.append(north + south)
                odd.append(north - south)
            for c in range(per_field):
                row = (field * per_field + c) * slots
                cut = slice(c * lat_rows, (c + 1) * lat_rows)
                (even_in0, even_in1)[h][row : row + slots, :] = jnp.concatenate([e[:, cut] for e in even], axis=1)
                (odd_in0, odd_in1)[h][row : row + slots, :] = jnp.concatenate([o[:, cut] for o in odd], axis=1)

    for slot in range(slots):
        picked = pl.ds(slot, columns, stride=slots)
        gain = 2.0 if slot else jnp.where(device == 0, 1.0, 2.0)
        weights = weight_ref[...] * gain
        found = []
        for parity, pair in enumerate(((even_in0, even_in1), (odd_in0, odd_in1))):
            values = jnp.concatenate([pair[0][picked, :], pair[1][picked, :]], axis=1) * weights
            if with_mass and slot == 0 and parity == 0:
                mass = jnp.sum(values, axis=1, keepdims=True)
            count = table_rows(degrees, devices, slot)
            offset = table_offset(degrees, devices, slot, parity)
            high, low = high_ref[offset : offset + count, :], low_ref[offset : offset + count, :]
            packed = pair_rows(values)
            coef = dot_nt(packed, high) + dot_nt(packed, low)
            level = degrees // 2 - count
            coef = (coef[:columns] + coef[columns:]) * heat_ref[parity : parity + 1, level:]
            packed = pair_rows(coef)
            back = dot_nn(packed, high) + dot_nn(packed, low)
            found.append(back[:columns] + back[columns:])
        north, south = found[0] + found[1], (found[0] - found[1]) * sign
        if with_mass and slot == 0:
            spread = jnp.broadcast_to(mass, north.shape)
            spread = pltpu.roll(spread, members, 0)
            which = lax.broadcasted_iota(jnp.int32, north.shape, 0) % per_field
            spare = (which >= members) & (device == 0)
            north, south = jnp.where(spare, spread, north), jnp.where(spare, spread, south)
        north0[picked, :], north1[picked, :] = north[:, :128], north[:, 128:]
        south0[picked, :], south1[picked, :] = south[:, :128], south[:, 128:]

    for field in range(fields):
        for lat in range(half_groups):
            h, q = lat // group_lanes, lat % group_lanes
            cut = slice(q * lat_rows, (q + 1) * lat_rows)
            rows = [(field * per_field + c) * slots for c in range(per_field)]
            north = [(north0, north1)[h][row : row + slots, cut] for row in rows]
            south = [(south0, south1)[h][row : row + slots, cut] for row in rows]
            out_ref[lat * fields + field] = jnp.concatenate(north, axis=1)
            out_ref[(lat_groups - 1 - lat) * fields + field] = jnp.concatenate(south, axis=1)


def on_device_packed(precip):
    lat_groups, fields = lax.axis_size("lat"), lax.axis_size("field")
    devices = lat_groups * fields
    members, lat_rows, lon_total = precip.shape
    lat_total, degrees = lat_rows * lat_groups, lon_total // 2
    slots = degrees // devices
    rows = members * lat_rows
    lat_index = lax.axis_index("lat")
    device = lat_index * fields + lax.axis_index("field")
    south = (lat_index >= lat_groups // 2).astype(jnp.int32)
    dev = jnp.stack([device.astype(jnp.int32), south])

    polar = np.pi * (np.arange(lat_total // 2) + 0.5) / lat_total
    weights = (np.sin(polar) * (np.pi / lat_total) * (2.0 * np.pi / lon_total)).astype(np.float32)[None]
    place = np.stack([np.cos(polar), np.log(np.sin(polar))]).astype(np.float32)
    level = np.arange(degrees)
    heat = np.exp(-heat_rate * level * (level + 1.0) / (degrees * (degrees - 1.0)))
    heat = heat.reshape(degrees // 2, 2).T.astype(np.float32)
    step = np.arange(1, degrees)
    starts = np.concatenate([[0.0], np.cumsum(np.log((2.0 * step - 1.0) / (2.0 * step)))])
    starts = 0.5 * np.log((2.0 * level + 1.0) / (4.0 * np.pi)) + 0.5 * starts
    starts = np.pad(starts.reshape(slots, devices), ((0, 0), (0, 128 - devices))).astype(np.float32)
    wave_high, wave_low = (jnp.asarray(t) for t in wave_tables(lon_total, devices, slots))

    vmem = pl.BlockSpec(memory_space=pltpu.VMEM)
    smem = pl.BlockSpec(memory_space=pltpu.SMEM)
    outer = devices // QUART
    spec_shape = jax.ShapeDtypeStruct((outer, QUART, slots, 2 * rows), jnp.float32)
    grid_shape = jax.ShapeDtypeStruct((rows, lon_total), jnp.float32)
    sum_shape = jax.ShapeDtypeStruct((lat_rows, lon_total), jnp.float32)
    table_total = table_offset(degrees, devices, slots, 0)
    table_shape = jax.ShapeDtypeStruct((table_total, lat_total // 2), jnp.bfloat16)

    def call(body, shapes, *operands, scratch=(), cost=None, name=None):
        return pl.pallas_call(
            body,
            out_shape=shapes,
            in_specs=[smem if o is dev else vmem for o in operands],
            out_specs=jax.tree.map(lambda _: vmem, shapes),
            scratch_shapes=list(scratch),
            cost_estimate=cost,
            compiler_params=pltpu.CompilerParams(vmem_limit_bytes=48 << 20),
            name=name,
        )(*operands)

    def exchange(spec):
        flat = spec.reshape(devices, slots, 2 * rows)
        return lax.all_to_all(flat, ("lat", "field"), split_axis=0, concat_axis=0, tiled=True)

    def swap(value):
        return lax.ppermute(value, "field", [(0, 1), (1, 0)])

    scratch128 = lambda count: pltpu.VMEM((count, 128), jnp.float32)

    def sphere(spec, with_mass):
        columns = fields * 2 * members

        def body(*refs):
            sphere_body(degrees, devices, slots, lat_groups, lat_rows, members, with_mass, *refs)

        shape = jax.ShapeDtypeStruct((devices, slots, 2 * rows), jnp.float32)
        done = call(
            body, shape, dev, exchange(spec), table_high, table_low, jnp.asarray(weights), jnp.asarray(heat),
            scratch=[scratch128(columns * slots)] * 8, name="sphere",
        )
        return exchange(done).reshape(spec_shape.shape)

    def bind(body, *fixed):
        return lambda *refs: body(*fixed, *refs)

    table_high, table_low = call(
        bind(legendre_body, degrees, devices, slots), (table_shape, table_shape), dev, jnp.asarray(place),
        jnp.asarray(starts),
        scratch=[pltpu.VMEM((slots, degrees), jnp.float32)] * 2 + [scratch128(degrees * slots)] * 2,
        cost=pl.CostEstimate(flops=40_000_000, bytes_accessed=16 << 20, transcendentals=0), name="legendre",
    )
    flipped, spec = call(
        bind(first_body, lat_rows), (grid_shape, spec_shape), dev, precip.reshape(rows, lon_total),
        wave_high, wave_low, name="first",
    )
    clamped, total, scaled = call(
        bind(mass_body, lat_rows), (grid_shape, sum_shape, grid_shape), sphere(spec, True), flipped,
        wave_high, wave_low, name="mass",
    )
    count = float(members * fields)
    logs, spec = call(
        bind(center_body, count, lat_rows), (grid_shape, spec_shape), clamped, total, swap(total),
        wave_high, wave_low, name="center",
    )
    spec = call(ratio_body, spec_shape, sphere(spec, False), scaled, wave_high, wave_low, name="ratio")
    clamped, total = call(
        bind(last_body, lat_rows), (grid_shape, sum_shape), dev, sphere(spec, False), logs, wave_high, wave_low,
        scratch=[pltpu.VMEM((rows, lon_total), jnp.float32), pltpu.VMEM((lat_rows, lon_total), jnp.float32)],
        name="last",
    )
    center = (total + swap(total)) / count
    return jnp.exp(center), center[None] - clamped.reshape(precip.shape)


def fits_packed(mesh, shape):
    lat_groups, fields = mesh.shape["lat"], mesh.shape["field"]
    devices = lat_groups * fields
    field_total, lat_total, lon_total = shape
    degrees = lon_total // 2
    members, lat_rows = field_total // fields, lat_total // lat_groups
    return (
        fields == 2
        and lon_total == 4 * lat_total // 2
        and lat_total == 512
        and 2 * members * lat_rows == 128
        and fields * 2 * members == 8
        and lat_groups % 2 == 0
        and devices % QUART == 0
        and degrees % (8 * devices) == 0
        and (devices // 2) % 16 == 0
        and devices <= 128
    )


def on_device(mesh, precip):
    members, lat_rows, lon_total = precip.shape
    shape = (members * mesh.shape["field"], lat_rows * mesh.shape["lat"], lon_total)
    return on_device_packed(precip) if ITERS == 2 and fits_packed(mesh, shape) else on_device_plain(precip)


def solution(mesh):
    in_specs = (P("field", "lat", None),)
    out_specs = (P("lat", None), P("field", "lat", None))
    return jax.shard_map(
        lambda precip: on_device(mesh, precip),
        mesh=mesh, in_specs=in_specs, out_specs=out_specs, check_vma=False,
    )
```

profile of v0, /device:TPU:0, one launch (start us, length us, event | category | flops | bytes accessed | tf_op | source)
XLA Modules:
  0.0 123.2 jit_solution(6173667006885438471)
XLA Ops:
  0.6 0.1 pad_add_fusion.refs_0_
  0.7 1.0 copy-done.3
  1.8 1.0 copy-done.5
  2.8 0.9 copy-done.7
  3.7 1.9 %first.1 = (f32[64,1024]{1,0:T(8,128)S(1)}, f32[8,4,16,128]{3,2,1,0:T(8,128)}) custom-call(s32[2]{0:T(128)S(1)} %pad_add_fusion.refs_0_, f32[64,1024]{1,0:T(8,128)S(1)} %bitcast.14, bf16[4,256,256]{2,1,0:T(8,128)(2,1)S(1)} %copy-done.5, bf16[4,256,256]{2,1,0:T(8,128)(2,1)S(1)} %copy-done.3), custom_call_target="tpu_custom_call" | custom-call | tf_op jit(solution)/shard_map/first/pallas_call | solution.py:507
  5.7 7.3 %all-to-all-start = ((f32[32,16,128]{2,1,0:T(8,128)}), f32[32,16,128]{2,1,0:T(8,128)S(1)}, u32[]{:S(2)}, u32[]{:S(2)}) async-start(f32[32,16,128]{2,1,0:T(8,128)} %bitcast.3), calls=%async_computation | async-start | bytes 524288 | tf_op jit(solution)/shard_map/all_to_all | solution.py:520
  13.0 0.7 copy-done.11
  13.7 0.7 copy-done.12
  14.4 6.1 %legendre.1 = (bf16[4352,256]{1,0:T(8,128)(2,1)S(1)}, bf16[4352,256]{1,0:T(8,128)(2,1)S(1)}) custom-call(s32[2]{0:T(128)S(1)} %pad_add_fusion.refs_0_, f32[2,256]{1,0:T(2,128)S(1)} %copy-done.12, f32[16,128]{1,0:T(8,128)S(1)} %copy-done.11), custom_call_target="tpu_custom_call" | custom-call | flops 40000000 | bytes 16777216 | tf_op jit(solution)/shard_map/legendre/pallas_call | solution.py:507
  20.5 1.4 %copy-done = bf16[4352,256]{1,0:T(8,128)(2,1)} copy-done((bf16[4352,256]{1,0:T(8,128)(2,1)}, bf16[4352,256]{1,0:T(8,128)(2,1)S(1)}, u32[]{:S(2)}) %copy-start) | copy-done | bytes 2228248
  21.8 1.7 %all-to-all-done.refs_1_ = f32[32,16,128]{2,1,0:T(8,128)S(1)} async-done(((f32[32,16,128]{2,1,0:T(8,128)}), f32[32,16,128]{2,1,0:T(8,128)S(1)}, u32[]{:S(2)}, u32[]{:S(2)}) %all-to-all-start) | async-done | bytes 262176 | tf_op jit(solution)/shard_map/all_to_all | solution.py:520
  23.6 1.6 %copy-done.1 = bf16[4352,256]{1,0:T(8,128)(2,1)S(1)} copy-done((bf16[4352,256]{1,0:T(8,128)(2,1)S(1)}, bf16[4352,256]{1,0:T(8,128)(2,1)}, u32[]{:S(2)}) %copy-start.1) | copy-done | bytes 2228248
  25.2 0.7 copy-done.8
  25.9 0.7 copy-done.10
  26.6 7.8 %sphere.3 = f32[32,16,128]{2,1,0:T(8,128)S(1)} custom-call(s32[2]{0:T(128)S(1)} %pad_add_fusion.refs_0_, f32[32,16,128]{2,1,0:T(8,128)S(1)} %all-to-all-done.refs_1_, bf16[4352,256]{1,0:T(8,128)(2,1)S(1)} %get-tuple-element.14.refs_2_, bf16[4352,256]{1,0:T(8,128)(2,1)S(1)} %copy-done.1, f32[1,256]{1,0:T(1,128)S(1)} %copy-done.10, f32[2,256]{1,0:T(2,128)S(1)} %copy-done.8), custom_call_target="tpu_custom_call" | custom-call | tf_op jit(solution)/shard_map/sphere/pallas_call | solution.py:507
  34.4 14.5 %all_to_all.30 = f32[32,16,128]{2,1,0:T(8,128)S(1)} all-to-all(f32[32,16,128]{2,1,0:T(8,128)S(1)} %sphere.3), channel_id=1, replica_groups=mesh['lat'=16,'field'=2] {'lat','field'}, dimensions={0} | all-to-all | bytes 524288 | tf_op jit(solution)/shard_map/all_to_all | solution.py:520
  48.9 0.5 mass.1
  49.4 0.1 collective-permute-start
  49.5 1.3 %collective-permute-done.refs_2_ = f32[32,1024]{1,0:T(8,128)S(1)} collective-permute-done((f32[32,1024]{1,0:T(8,128)S(1)}, f32[32,1024]{1,0:T(8,128)S(1)}, u32[]{:S(2)}, u32[]{:S(2)}) %collective-permute-start) | collective-permute-done | bytes 131104 | tf_op jit(solution)/shard_map/ppermute | solution.py:523
  50.8 0.6 center.1
  51.4 12.8 %all_to_all.31.refs_1_ = f32[32,16,128]{2,1,0:T(8,128)S(1)} all-to-all(f32[32,16,128]{2,1,0:T(8,128)S(1)} %bitcast.16), channel_id=1, replica_groups=mesh['lat'=16,'field'=2] {'lat','field'}, dimensions={0} | all-to-all | bytes 524288 | tf_op jit(solution)/shard_map/all_to_all | solution.py:520
  64.2 7.8 %sphere.4 = f32[32,16,128]{2,1,0:T(8,128)S(1)} custom-call(s32[2]{0:T(128)S(1)} %pad_add_fusion.refs_0_, f32[32,16,128]{2,1,0:T(8,128)S(1)} %all_to_all.31.refs_1_, bf16[4352,256]{1,0:T(8,128)(2,1)S(1)} %get-tuple-element.14.refs_2_, bf16[4352,256]{1,0:T(8,128)(2,1)S(1)} %copy-done.2, f32[1,256]{1,0:T(1,128)S(1)} %copy-done.10, f32[2,256]{1,0:T(2,128)S(1)} %copy-done.9), custom_call_target="tpu_custom_call" | custom-call | tf_op jit(solution)/shard_map/sphere/pallas_call | solution.py:507
  72.0 12.8 %all_to_all.32 = f32[32,16,128]{2,1,0:T(8,128)S(1)} all-to-all(f32[32,16,128]{2,1,0:T(8,128)S(1)} %sphere.4), channel_id=1, replica_groups=mesh['lat'=16,'field'=2] {'lat','field'}, dimensions={0} | all-to-all | bytes 524288 | tf_op jit(solution)/shard_map/all_to_all | solution.py:520
  84.8 1.0 ratio.1
  85.8 12.8 %all_to_all.33.refs_1_ = f32[32,16,128]{2,1,0:T(8,128)S(1)} all-to-all(f32[32,16,128]{2,1,0:T(8,128)S(1)} %bitcast.11), channel_id=1, replica_groups=mesh['lat'=16,'field'=2] {'lat','field'}, dimensions={0} | all-to-all | bytes 524288 | tf_op jit(solution)/shard_map/all_to_all | solution.py:520
  98.6 7.8 %sphere.5 = f32[32,16,128]{2,1,0:T(8,128)S(1)} custom-call(s32[2]{0:T(128)S(1)} %pad_add_fusion.refs_0_, f32[32,16,128]{2,1,0:T(8,128)S(1)} %all_to_all.33.refs_1_, bf16[4352,256]{1,0:T(8,128)(2,1)S(1)} %get-tuple-element.14.refs_2_, bf16[4352,256]{1,0:T(8,128)(2,1)S(1)} %copy-done.2, f32[1,256]{1,0:T(1,128)S(1)} %copy-done.10, f32[2,256]{1,0:T(2,128)S(1)} %copy-done.9), custom_call_target="tpu_custom_call" | custom-call | tf_op jit(solution)/shard_map/sphere/pallas_call | solution.py:507
  106.4 12.8 %all_to_all.34 = f32[32,16,128]{2,1,0:T(8,128)S(1)} all-to-all(f32[32,16,128]{2,1,0:T(8,128)S(1)} %sphere.5), channel_id=1, replica_groups=mesh['lat'=16,'field'=2] {'lat','field'}, dimensions={0} | all-to-all | bytes 524288 | tf_op jit(solution)/shard_map/all_to_all | solution.py:520
  119.2 1.2 last.1
  120.3 0.1 collective-permute-start.1
  120.4 1.3 %collective-permute-done.1 = f32[32,1024]{1,0:T(8,128)S(1)} collective-permute-done((f32[32,1024]{1,0:T(8,128)S(1)}, f32[32,1024]{1,0:T(8,128)S(1)}, u32[]{:S(2)}, u32[]{:S(2)}) %collective-permute-start.1) | collective-permute-done | bytes 131104 | tf_op jit(solution)/shard_map/ppermute | solution.py:523
  121.8 0.7 fusion
  122.4 0.7 broadcast_subtract_fusion
  (17 shorter events, 0.0 us)
Async XLA Ops:
  0.7 1.0 copy-start.3
  1.8 1.0 copy-start.5
  2.8 0.9 copy-start.7
  5.7 17.9 %all-to-all-start = ((f32[32,16,128]{2,1,0:T(8,128)}), f32[32,16,128]{2,1,0:T(8,128)S(1)}, u32[]{:S(2)}, u32[]{:S(2)}) async-start(f32[32,16,128]{2,1,0:T(8,128)} %bitcast.3), calls=%async_computation | async-start | bytes 524288 | tf_op jit(solution)/shard_map/all_to_all | solution.py:520
  13.0 0.7 copy-start.11
  13.7 0.7 copy-start.12
  20.4 1.4 %copy-start = (bf16[4352,256]{1,0:T(8,128)(2,1)}, bf16[4352,256]{1,0:T(8,128)(2,1)S(1)}, u32[]{:S(2)}) copy-start(bf16[4352,256]{1,0:T(8,128)(2,1)S(1)} %get-tuple-element.15.refs_3_) | copy-start | bytes 6684676
  23.6 1.6 %copy-start.1 = (bf16[4352,256]{1,0:T(8,128)(2,1)S(1)}, bf16[4352,256]{1,0:T(8,128)(2,1)}, u32[]{:S(2)}) copy-start(bf16[4352,256]{1,0:T(8,128)(2,1)} %copy-done) | copy-start | bytes 6684676
  25.2 0.7 copy-start.8
  25.9 0.7 copy-start.10
  26.6 22.3 %copy-start.4 = (bf16[4,256,256]{2,1,0:T(8,128)(2,1)S(1)}, bf16[4,256,256]{2,1,0:T(8,128)(2,1)}, u32[]{:S(2)}) copy-start(bf16[4,256,256]{2,1,0:T(8,128)(2,1)} %constant.28.clone.refs_3_.refs_4_.low_ref) | copy-start | bytes 1572868
  26.6 22.3 %copy-start.6 = (bf16[4,256,256]{2,1,0:T(8,128)(2,1)S(1)}, bf16[4,256,256]{2,1,0:T(8,128)(2,1)}, u32[]{:S(2)}) copy-start(bf16[4,256,256]{2,1,0:T(8,128)(2,1)} %constant.27.clone.refs_2_.refs_3_.high_ref) | copy-start | bytes 1572868
  34.3 29.9 %copy-start.2 = (bf16[4352,256]{1,0:T(8,128)(2,1)S(1)}, bf16[4352,256]{1,0:T(8,128)(2,1)}, u32[]{:S(2)}) copy-start(bf16[4352,256]{1,0:T(8,128)(2,1)} %copy-done) | copy-start | bytes 6684676
  34.3 29.8 %copy-start.9 = (f32[2,256]{1,0:T(2,128)S(1)}, f32[2,256]{1,0:T(2,128)}, u32[]{:S(2)}) copy-start(f32[2,256]{1,0:T(2,128)} %constant.32.clone.refs_5_) | copy-start | bytes 6148
  49.4 1.4 %collective-permute-start = (f32[32,1024]{1,0:T(8,128)S(1)}, f32[32,1024]{1,0:T(8,128)S(1)}, u32[]{:S(2)}, u32[]{:S(2)}) collective-permute-start(f32[32,1024]{1,0:T(8,128)S(1)} %get-tuple-element.18.refs_1_), channel_id=1, source_target_pairs={{0,1},{1,0},{2,3},{3,2},{4,5},{5,4},{6,7},{7,6},{8,9},{9,8},{10,11... | collective-permute-start | bytes 393224 | tf_op jit(solution)/shard_map/ppermute | solution.py:523
  120.3 1.4 %collective-permute-start.1 = (f32[32,1024]{1,0:T(8,128)S(1)}, f32[32,1024]{1,0:T(8,128)S(1)}, u32[]{:S(2)}, u32[]{:S(2)}) collective-permute-start(f32[32,1024]{1,0:T(8,128)S(1)} %get-tuple-element.22), channel_id=1, source_target_pairs={{0,1},{1,0},{2,3},{3,2},{4,5},{5,4},{6,7},{7,6},{8,9},{9,8},{10,11... | collective-permute-start | bytes 393224 | tf_op jit(solution)/shard_map/ppermute | solution.py:523
where the time goes:
time: 124 us; the launch traced here: 123 us
  blocking collectives  65.8 us (53%)
  Pallas kernels  34.5 us (28%)
  local copies, waits for them, and re-layouts  8.8 us (7%)
  starting transfers between devices  7.44 us (6%)
  waiting for transfers between devices  4.4 us (4%)
  other arithmetic  1.49 us (1%)
    all_to_all x5, blocking collectives, exchange(): lax.all_to_all(flat, ('lat', 'field'), split_axis=0, concat_axis=0, tiled...  65.8 us
    pallas_call x9, Pallas kernels, call(): pl.pallas_call(body, out_shape=shapes, in_specs=[smem if o is dev else vm...  34.5 us
    unnamed x26, local copies, waits for them, and re-layouts  8.8 us
    all_to_all x1, starting transfers between devices, exchange(): lax.all_to_all(flat, ('lat', 'field'), split_axis=0, concat_axis=0, tiled...  7.3 us
    ppermute x2, waiting for transfers between devices, swap(): return lax.ppermute(value, 'field', [(0, 1), (1, 0)])  2.67 us
  transfers between devices with their start and end apart: 3, of which 3 were waited for; matrix products, arithmetic and copies ran while one was open for 0% of the time, Pallas kernels for 5%

commit v1 on v0

--- a/solution.py
+++ b/solution.py
@@ -212,10 +212,10 @@
     table = np.concatenate([np.cos(phase), np.sin(phase)], axis=1).astype(np.float32)
     high = table.astype(ml_dtypes.bfloat16)
     low = (table - high.astype(np.float32)).astype(ml_dtypes.bfloat16)
-    return high, low
-
-
-def forward_waves(field, high_ref, low_ref, out_ref):
+    return np.stack([high, low])
+
+
+def forward_waves(field, wave_ref, out_ref, ready=None, done=None):
     span = field.shape[1] // QUART
     rows = field.shape[0]
     lanes = 2 * rows
@@ -224,11 +224,13 @@
     diff_even, diff_odd = part[0] - part[2], part[1] - part[3]
     stack_even = pair_rows(jnp.concatenate([sum_even + sum_odd, sum_even - sum_odd], axis=0))
     stack_odd = pair_rows(jnp.concatenate([diff_even, diff_odd], axis=0))
-    orders = high_ref.shape[1] // 2
+    orders = wave_ref.shape[2] // 2
     first = lax.broadcasted_iota(jnp.int32, (orders, lanes), 1) < rows
     for residue in range(QUART):
         stack = stack_odd if residue % 2 else stack_even
-        found = dot_nt(high_ref[residue], stack) + dot_nt(low_ref[residue], stack)
+        if ready:
+            ready[residue].wait()
+        found = dot_nt(wave_ref[0, residue], stack) + dot_nt(wave_ref[1, residue], stack)
         found = found[:, :lanes] + found[:, lanes:]
         cosine, sine = found[:orders], found[orders:]
         if residue == 0:
@@ -241,9 +243,11 @@
             turned = pltpu.roll(sine, rows, 1)
             packed = cosine + jnp.where(first, turned, -turned)
         out_ref[:, residue] = packed.reshape(out_ref.shape[0], out_ref.shape[2], lanes)
-
-
-def inverse_waves(spec_ref, high_ref, low_ref):
+        if done:
+            done[residue].start()
+
+
+def inverse_waves(spec_ref, wave_ref):
     outer, _, slots, lanes = spec_ref.shape
     rows = lanes // 2
     real = [None] * QUART
@@ -259,7 +263,7 @@
             left = jnp.concatenate([left, jnp.concatenate([sine, cosine], axis=1)], axis=0)
         count = left.shape[0]
         left = pair_rows(left)
-        found = dot_nn(left, high_ref[residue]) + dot_nn(left, low_ref[residue])
+        found = dot_nn(left, wave_ref[0, residue]) + dot_nn(left, wave_ref[1, residue])
         found = found[:count] + found[count:]
         real[residue] = found[:rows]
         if residue % 2:
@@ -269,17 +273,52 @@
     return jnp.concatenate([plus + both, minus - gap, plus - both, minus + gap], axis=1), spare
 
 
-def copy_flipped(src_ref, dst_ref, south, lat_rows):
-    rows = src_ref.shape[0]
-    for row in range(rows):
-        base, offset = row - row % lat_rows, row % lat_rows
-        target = base + jnp.where(south, lat_rows - 1 - offset, offset)
-        dst_ref[pl.ds(target, 1), :] = src_ref[row : row + 1, :]
-
-
-def first_body(lat_rows, dev_ref, field_ref, high_ref, low_ref, flipped_ref, out_ref):
-    copy_flipped(field_ref, flipped_ref, dev_ref[1] > 0, lat_rows)
-    forward_waves(flipped_ref[...], high_ref, low_ref, out_ref)
+def flip_rows(value, south, lat_rows):
+    lanes = 128
+    rows, width = value.shape
+    sub = lax.broadcasted_iota(jnp.int32, (8, lanes), 0)
+    source = jnp.where(south, 7 - sub, sub)
+    blocks = lat_rows // 8
+    out = []
+    for base in range(0, rows, lat_rows):
+        for block in range(blocks):
+            near = value[base + 8 * block : base + 8 * block + 8]
+            far = value[base + 8 * (blocks - 1 - block) : base + 8 * (blocks - block)]
+            tile = jnp.where(south, far, near)
+            pieces = [
+                jnp.take_along_axis(tile[:, at : at + lanes], source, axis=0) for at in range(0, width, lanes)
+            ]
+            out.append(jnp.concatenate(pieces, axis=1))
+    return jnp.concatenate(out, axis=0)
+
+
+def device_index():
+    return lax.axis_index("lat") * lax.axis_size("field") + lax.axis_index("field")
+
+
+def in_south():
+    return lax.axis_index("lat") >= lax.axis_size("lat") // 2
+
+
+def first_body(lat_rows, field_hbm, wave_hbm, flipped_hbm, out_hbm, field_ref, wave_ref, flipped_ref, out_ref, sems):
+    get_field = pltpu.make_async_copy(field_hbm, field_ref, sems.at[0])
+    get_wave = [
+        pltpu.make_async_copy(wave_hbm.at[:, r], wave_ref.at[:, r], sems.at[1 + r]) for r in range(QUART)
+    ]
+    put_flipped = pltpu.make_async_copy(flipped_ref, flipped_hbm, sems.at[1 + QUART])
+    put_wave = [
+        pltpu.make_async_copy(out_ref.at[:, r], out_hbm.at[:, r], sems.at[2 + QUART + r]) for r in range(QUART)
+    ]
+    get_field.start()
+    for copy in get_wave:
+        copy.start()
+    get_field.wait()
+    flipped_ref[...] = flip_rows(field_ref[...], in_south(), lat_rows)
+    put_flipped.start()
+    forward_waves(flipped_ref[...], wave_ref, out_ref, get_wave, put_wave)
+    put_flipped.wait()
+    for copy in put_wave:
+        copy.wait()
 
 
 def member_sum(value, lat_rows):
@@ -289,8 +328,8 @@
     return total
 
 
-def mass_body(lat_rows, spec_ref, field_ref, high_ref, low_ref, clamp_ref, sum_ref, scaled_ref):
-    blurred, total = inverse_waves(spec_ref, high_ref, low_ref)
+def mass_body(lat_rows, spec_ref, field_ref, wave_ref, clamp_ref, sum_ref, scaled_ref):
+    blurred, total = inverse_waves(spec_ref, wave_ref)
     inverse = (4.0 * math.pi) / total
     scaled_ref[...] = field_ref[...] * inverse
     clamped = jnp.log(jnp.maximum(blurred * inverse, floor_value))
@@ -298,26 +337,32 @@
     sum_ref[...] = member_sum(clamped, lat_rows)
 
 
-def center_body(count, lat_rows, clamp_ref, sum_ref, other_ref, high_ref, low_ref, logs_ref, out_ref):
+def center_body(count, lat_rows, clamp_ref, sum_ref, other_ref, wave_ref, logs_ref, out_ref):
     center = (sum_ref[...] + other_ref[...]) / count
     members = clamp_ref.shape[0] // lat_rows
     logs = jnp.concatenate([center] * members, axis=0) - clamp_ref[...]
     logs_ref[...] = logs
-    forward_waves(jnp.exp(logs), high_ref, low_ref, out_ref)
-
-
-def ratio_body(spec_ref, scaled_ref, high_ref, low_ref, out_ref):
-    blurred, _ = inverse_waves(spec_ref, high_ref, low_ref)
-    forward_waves(scaled_ref[...] / jnp.maximum(blurred, floor_value), high_ref, low_ref, out_ref)
-
-
-def last_body(lat_rows, dev_ref, spec_ref, logs_ref, high_ref, low_ref, clamp_ref, sum_ref, clamp_tmp, sum_tmp):
-    blurred, _ = inverse_waves(spec_ref, high_ref, low_ref)
+    forward_waves(jnp.exp(logs), wave_ref, out_ref)
+
+
+def ratio_body(spec_ref, scaled_ref, wave_ref, out_ref):
+    blurred, _ = inverse_waves(spec_ref, wave_ref)
+    forward_waves(scaled_ref[...] / jnp.maximum(blurred, floor_value), wave_ref, out_ref)
+
+
+def last_body(lat_rows, spec_ref, logs_ref, wave_ref, clamp_ref, sum_ref):
+    blurred, _ = inverse_waves(spec_ref, wave_ref)
     clamped = jnp.log(jnp.maximum(blurred, floor_value))
-    clamp_tmp[...] = clamped
-    sum_tmp[...] = member_sum(logs_ref[...] + clamped, lat_rows)
-    copy_flipped(clamp_tmp, clamp_ref, dev_ref[1] > 0, lat_rows)
-    copy_flipped(sum_tmp, sum_ref, dev_ref[1] > 0, lat_rows)
+    clamp_ref[...] = clamped
+    sum_ref[...] = member_sum(logs_ref[...] + clamped, lat_rows)
+
+
+def final_body(count, lat_rows, clamp_ref, sum_ref, other_ref, center_ref, logs_ref):
+    south = in_south()
+    center = flip_rows((sum_ref[...] + other_ref[...]) / count, south, lat_rows)
+    center_ref[...] = jnp.exp(center)
+    members = clamp_ref.shape[0] // lat_rows
+    logs_ref[...] = jnp.concatenate([center] * members, axis=0) - flip_rows(clamp_ref[...], south, lat_rows)
 
 
 def table_rows(degrees, devices, slot):
@@ -329,27 +374,44 @@
     return start + parity * table_rows(degrees, devices, slot)
 
 
-def legendre_body(degrees, devices, slots, dev_ref, place_ref, start_ref, high_ref, low_ref,
-                  first_coef, second_coef, left_half, right_half):
+FAR_SLOTS = 3
+
+
+def table_part(degrees, devices, slot, parity, near_ref, far_ref):
+    count = table_rows(degrees, devices, slot)
+    offset = table_offset(degrees, devices, slot, parity)
+    if slot < FAR_SLOTS:
+        return far_ref, offset, count
+    return near_ref, offset - table_offset(degrees, devices, FAR_SLOTS, 0), count
+
+
+def legendre_body(degrees, devices, slots, fixed_hbm, near_ref, far_hbm, fixed_ref, first_coef,
+                  second_coef, left_half, right_half, far_ref, sem, far_sem):
+    copy = pltpu.make_async_copy(fixed_hbm, fixed_ref, sem)
+    copy.start()
     half = (left_half, right_half)
     lanes = 128
-    device = dev_ref[0]
+    device = device_index()
     order = lax.broadcasted_iota(jnp.int32, (slots, degrees), 0) * devices + device
     level = lax.broadcasted_iota(jnp.int32, (slots, degrees), 1)
     above = level > order
     order, level = order.astype(jnp.float32), level.astype(jnp.float32)
     diff = jnp.maximum(level * level - order * order, 1.0)
-    first_coef[...] = jnp.where(above, jnp.sqrt((4.0 * level * level - 1.0) / diff), 0.0)
+    rate = 0.5 * heat_rate / (degrees * (degrees - 1.0))
+    first_ratio = jnp.exp(-rate * (2.0 * level))
+    second_ratio = jnp.exp(-rate * (4.0 * level - 2.0))
+    first_coef[...] = jnp.where(above, jnp.sqrt((4.0 * level * level - 1.0) / diff) * first_ratio, 0.0)
     numer = (2.0 * level + 1.0) * (level + order - 1.0) * (level - order - 1.0)
     denom = jnp.maximum((2.0 * level - 3.0) * diff, 1.0)
-    second_coef[...] = jnp.where(above, jnp.sqrt(jnp.maximum(numer, 0.0) / denom), 0.0)
+    second_coef[...] = jnp.where(above, jnp.sqrt(jnp.maximum(numer, 0.0) / denom) * second_ratio, 0.0)
+    copy.wait()
 
     lane = lax.broadcasted_iota(jnp.int32, (slots, lanes), 1)
-    start = jnp.sum(jnp.where(lane == device, start_ref[...], 0.0), axis=1, keepdims=True)
+    start = jnp.sum(jnp.where(lane == device, fixed_ref[0:slots, 0:lanes], 0.0), axis=1, keepdims=True)
     sub = lax.broadcasted_iota(jnp.int32, (8, lanes), 0)
     tiles = slots // 8
-    cosine = [jnp.broadcast_to(place_ref[0:1, h * lanes : (h + 1) * lanes], (8, lanes)) for h in range(2)]
-    log_sine = [jnp.broadcast_to(place_ref[1:2, h * lanes : (h + 1) * lanes], (8, lanes)) for h in range(2)]
+    cosine = [jnp.broadcast_to(fixed_ref[slots : slots + 1, h * lanes : (h + 1) * lanes], (8, lanes)) for h in range(2)]
+    log_sine = [jnp.broadcast_to(fixed_ref[slots + 1 : slots + 2, h * lanes : (h + 1) * lanes], (8, lanes)) for h in range(2)]
     order_tile = [(sub + 8 * t) * devices + device for t in range(tiles)]
     zero = jnp.zeros((8, lanes), jnp.float32)
     span_log = 60.0 * math.log(2.0)
@@ -394,26 +456,21 @@
             states.append(fresh(len(states)))
         states = chunk(index, states)
 
+    put_far = pltpu.make_async_copy(far_ref, far_hbm, far_sem)
     for slot in range(slots):
-        count = table_rows(degrees, devices, slot)
         for parity in range(2):
-            offset = table_offset(degrees, devices, slot, parity)
+            part_ref, offset, count = table_part(degrees, devices, slot, parity, near_ref, far_ref)
             begin = (devices * slot + parity) * slots + slot
             for h in range(2):
                 high, low = split_pair(half[h][pl.ds(begin, count, stride=2 * slots), :])
-                high_ref[offset : offset + count, h * lanes : (h + 1) * lanes] = high
-                low_ref[offset : offset + count, h * lanes : (h + 1) * lanes] = low
-
-
-def sphere_body(degrees, devices, slots, lat_groups, lat_rows, members, with_mass, dev_ref, spec_ref, high_ref,
-                low_ref, weight_ref, heat_ref, out_ref, even_in0, even_in1, odd_in0, odd_in1,
-                north0, north1, south0, south1):
-    device = dev_ref[0]
-    sign = jnp.where(device % 2 == 0, 1.0, -1.0)
-    fields = devices // lat_groups
-    half_groups = lat_groups // 2
-    per_field = 2 * members
-    columns = fields * per_field
+                part_ref[0, offset : offset + count, h * lanes : (h + 1) * lanes] = high
+                part_ref[1, offset : offset + count, h * lanes : (h + 1) * lanes] = low
+        if slot == FAR_SLOTS - 1:
+            put_far.start()
+    put_far.wait()
+
+
+def gather_orders(spec_ref, sign, fields, lat_groups, lat_rows, per_field, slots, even_in, odd_in):
     group_lanes = 128 // lat_rows
     for field in range(fields):
         for h in range(2):
@@ -427,26 +484,70 @@
             for c in range(per_field):
                 row = (field * per_field + c) * slots
                 cut = slice(c * lat_rows, (c + 1) * lat_rows)
-                (even_in0, even_in1)[h][row : row + slots, :] = jnp.concatenate([e[:, cut] for e in even], axis=1)
-                (odd_in0, odd_in1)[h][row : row + slots, :] = jnp.concatenate([o[:, cut] for o in odd], axis=1)
-
-    for slot in range(slots):
+                even_in[h][row : row + slots, :] = jnp.concatenate([e[:, cut] for e in even], axis=1)
+                odd_in[h][row : row + slots, :] = jnp.concatenate([o[:, cut] for o in odd], axis=1)
+
+
+def scatter_orders(out_ref, fields, lat_groups, lat_rows, per_field, slots, north, south):
+    group_lanes = 128 // lat_rows
+    for field in range(fields):
+        for lat in range(lat_groups // 2):
+            h, q = lat // group_lanes, lat % group_lanes
+            cut = slice(q * lat_rows, (q + 1) * lat_rows)
+            rows = [(field * per_field + c) * slots for c in range(per_field)]
+            near = [north[h][row : row + slots, cut] for row in rows]
+            far = [south[h][row : row + slots, cut] for row in rows]
+            out_ref[lat * fields + field] = jnp.concatenate(near, axis=1)
+            out_ref[(lat_groups - 1 - lat) * fields + field] = jnp.concatenate(far, axis=1)
+
+
+def sphere_body(degrees, devices, slots, lat_groups, lat_rows, members, with_mass, spec_ref, near_ref, far_in,
+                fixed_hbm, out_ref, *rest):
+    far_ref, rest = (rest[0], rest[1:]) if with_mass else (far_in, rest)
+    fixed_ref, coef_ref, sem, far_sem = rest[:4]
+    halves = rest[4:]
+    copy = pltpu.make_async_copy(fixed_hbm, fixed_ref, sem)
+    copy.start()
+    if with_mass:
+        get_far = pltpu.make_async_copy(far_in, far_ref, far_sem)
+        get_far.start()
+    even_in, odd_in, north_out, south_out = halves[0:2], halves[2:4], halves[4:6], halves[6:8]
+    device = device_index()
+    sign = jnp.where(device % 2 == 0, 1.0, -1.0)
+    fields = devices // lat_groups
+    per_field = 2 * members
+    columns = fields * per_field
+    gather_orders(spec_ref, sign, fields, lat_groups, lat_rows, per_field, slots, even_in, odd_in)
+    copy.wait()
+    mass = None
+
+    def pick(slot, parity):
         picked = pl.ds(slot, columns, stride=slots)
         gain = 2.0 if slot else jnp.where(device == 0, 1.0, 2.0)
-        weights = weight_ref[...] * gain
+        pair = (even_in, odd_in)[parity]
+        values = jnp.concatenate([pair[0][picked, :], pair[1][picked, :]], axis=1)
+        return values * (fixed_ref[slots + 2 : slots + 3, :] * gain)
+
+    def table(slot, parity):
+        part_ref, offset, count = table_part(degrees, devices, slot, parity, near_ref, far_ref)
+        return part_ref[0, offset : offset + count, :], part_ref[1, offset : offset + count, :], count
+
+    if with_mass:
+        mass = jnp.sum(pick(0, 0), axis=1, keepdims=True)
+    for slot in list(range(FAR_SLOTS, slots)) + list(range(FAR_SLOTS)):
+        if with_mass and slot == 0:
+            get_far.wait()
+        for parity in range(2):
+            high, low, count = table(slot, parity)
+            packed = pair_rows(pick(slot, parity))
+            coef = dot_nt(packed, high) + dot_nt(packed, low)
+            coef_ref[2 * slot + parity, :, 0:count] = pair_rows(coef[:columns] + coef[columns:])
+
+    for slot in range(slots):
         found = []
-        for parity, pair in enumerate(((even_in0, even_in1), (odd_in0, odd_in1))):
-            values = jnp.concatenate([pair[0][picked, :], pair[1][picked, :]], axis=1) * weights
-            if with_mass and slot == 0 and parity == 0:
-                mass = jnp.sum(values, axis=1, keepdims=True)
-            count = table_rows(degrees, devices, slot)
-            offset = table_offset(degrees, devices, slot, parity)
-            high, low = high_ref[offset : offset + count, :], low_ref[offset : offset + count, :]
-            packed = pair_rows(values)
-            coef = dot_nt(packed, high) + dot_nt(packed, low)
-            level = degrees // 2 - count
-            coef = (coef[:columns] + coef[columns:]) * heat_ref[parity : parity + 1, level:]
-            packed = pair_rows(coef)
+        for parity in range(2):
+            high, low, count = table(slot, parity)
+            packed = coef_ref[2 * slot + parity, :, 0:count]
             back = dot_nn(packed, high) + dot_nn(packed, low)
             found.append(back[:columns] + back[columns:])
         north, south = found[0] + found[1], (found[0] - found[1]) * sign
@@ -456,18 +557,12 @@
             which = lax.broadcasted_iota(jnp.int32, north.shape, 0) % per_field
             spare = (which >= members) & (device == 0)
             north, south = jnp.where(spare, spread, north), jnp.where(spare, spread, south)
-        north0[picked, :], north1[picked, :] = north[:, :128], north[:, 128:]
-        south0[picked, :], south1[picked, :] = south[:, :128], south[:, 128:]
-
-    for field in range(fields):
-        for lat in range(half_groups):
-            h, q = lat // group_lanes, lat % group_lanes
-            cut = slice(q * lat_rows, (q + 1) * lat_rows)
-            rows = [(field * per_field + c) * slots for c in range(per_field)]
-            north = [(north0, north1)[h][row : row + slots, cut] for row in rows]
-            south = [(south0, south1)[h][row : row + slots, cut] for row in rows]
-            out_ref[lat * fields + field] = jnp.concatenate(north, axis=1)
-            out_ref[(lat_groups - 1 - lat) * fields + field] = jnp.concatenate(south, axis=1)
+        picked = pl.ds(slot, columns, stride=slots)
+        for h in range(2):
+            north_out[h][picked, :] = north[:, 128 * h : 128 * h + 128]
+            south_out[h][picked, :] = south[:, 128 * h : 128 * h + 128]
+
+    scatter_orders(out_ref, fields, lat_groups, lat_rows, per_field, slots, north_out, south_out)
 
 
 def on_device_packed(precip):
@@ -477,41 +572,43 @@
     lat_total, degrees = lat_rows * lat_groups, lon_total // 2
     slots = degrees // devices
     rows = members * lat_rows
-    lat_index = lax.axis_index("lat")
-    device = lat_index * fields + lax.axis_index("field")
-    south = (lat_index >= lat_groups // 2).astype(jnp.int32)
-    dev = jnp.stack([device.astype(jnp.int32), south])
-
     polar = np.pi * (np.arange(lat_total // 2) + 0.5) / lat_total
-    weights = (np.sin(polar) * (np.pi / lat_total) * (2.0 * np.pi / lon_total)).astype(np.float32)[None]
-    place = np.stack([np.cos(polar), np.log(np.sin(polar))]).astype(np.float32)
     level = np.arange(degrees)
-    heat = np.exp(-heat_rate * level * (level + 1.0) / (degrees * (degrees - 1.0)))
-    heat = heat.reshape(degrees // 2, 2).T.astype(np.float32)
     step = np.arange(1, degrees)
     starts = np.concatenate([[0.0], np.cumsum(np.log((2.0 * step - 1.0) / (2.0 * step)))])
     starts = 0.5 * np.log((2.0 * level + 1.0) / (4.0 * np.pi)) + 0.5 * starts
-    starts = np.pad(starts.reshape(slots, devices), ((0, 0), (0, 128 - devices))).astype(np.float32)
-    wave_high, wave_low = (jnp.asarray(t) for t in wave_tables(lon_total, devices, slots))
+    starts = starts - 0.5 * heat_rate * level * (level + 1.0) / (degrees * (degrees - 1.0))
+    fixed = np.zeros((slots + 8, lat_total // 2), np.float32)
+    fixed[:slots, :devices] = starts.reshape(slots, devices)
+    fixed[slots] = np.cos(polar)
+    fixed[slots + 1] = np.log(np.sin(polar))
+    fixed[slots + 2] = np.sin(polar) * (np.pi / lat_total) * (2.0 * np.pi / lon_total)
+    fixed = jnp.asarray(fixed)
+    wave = jnp.asarray(wave_tables(lon_total, devices, slots))
 
     vmem = pl.BlockSpec(memory_space=pltpu.VMEM)
-    smem = pl.BlockSpec(memory_space=pltpu.SMEM)
     outer = devices // QUART
     spec_shape = jax.ShapeDtypeStruct((outer, QUART, slots, 2 * rows), jnp.float32)
     grid_shape = jax.ShapeDtypeStruct((rows, lon_total), jnp.float32)
     sum_shape = jax.ShapeDtypeStruct((lat_rows, lon_total), jnp.float32)
-    table_total = table_offset(degrees, devices, slots, 0)
-    table_shape = jax.ShapeDtypeStruct((table_total, lat_total // 2), jnp.bfloat16)
-
-    def call(body, shapes, *operands, scratch=(), cost=None, name=None):
+    far_rows = table_offset(degrees, devices, FAR_SLOTS, 0)
+    near_rows = table_offset(degrees, devices, slots, 0) - far_rows
+    near_shape = jax.ShapeDtypeStruct((2, near_rows, lat_total // 2), jnp.bfloat16)
+    far_shape = jax.ShapeDtypeStruct((2, far_rows, lat_total // 2), jnp.bfloat16)
+    flat_shape = jax.ShapeDtypeStruct((devices, slots, 2 * rows), jnp.float32)
+    hbm = pl.BlockSpec(memory_space=pl.ANY)
+
+    def call(body, shapes, *operands, name, far=(), far_out=(), scratch=(), cost=None, limit=8):
+        single = not isinstance(shapes, tuple)
+        outs = [hbm if index in far_out else vmem for index in range(1 if single else len(shapes))]
         return pl.pallas_call(
             body,
             out_shape=shapes,
-            in_specs=[smem if o is dev else vmem for o in operands],
-            out_specs=jax.tree.map(lambda _: vmem, shapes),
+            in_specs=[hbm if any(o is f for f in far) else vmem for o in operands],
+            out_specs=outs[0] if single else outs,
             scratch_shapes=list(scratch),
             cost_estimate=cost,
-            compiler_params=pltpu.CompilerParams(vmem_limit_bytes=48 << 20),
+            compiler_params=pltpu.CompilerParams(vmem_limit_bytes=limit << 20),
             name=name,
         )(*operands)
 
@@ -522,51 +619,61 @@
     def swap(value):
         return lax.ppermute(value, "field", [(0, 1), (1, 0)])
 
-    scratch128 = lambda count: pltpu.VMEM((count, 128), jnp.float32)
-
-    def sphere(spec, with_mass):
-        columns = fields * 2 * members
-
-        def body(*refs):
-            sphere_body(degrees, devices, slots, lat_groups, lat_rows, members, with_mass, *refs)
-
-        shape = jax.ShapeDtypeStruct((devices, slots, 2 * rows), jnp.float32)
-        done = call(
-            body, shape, dev, exchange(spec), table_high, table_low, jnp.asarray(weights), jnp.asarray(heat),
-            scratch=[scratch128(columns * slots)] * 8, name="sphere",
+    def bind(body, *bound):
+        return lambda *refs: body(*bound, *refs)
+
+    def buffer(shape, dtype=jnp.float32):
+        return pltpu.VMEM(shape, dtype)
+
+    columns = fields * 2 * members
+    signal = pltpu.SemaphoreType.DMA(())
+
+    def sphere(spec, near, far, with_mass):
+        return call(
+            bind(sphere_body, degrees, devices, slots, lat_groups, lat_rows, members, with_mass),
+            (flat_shape, far_shape) if with_mass else flat_shape,
+            exchange(spec), near, far, fixed, far=(far, fixed) if with_mass else (fixed,), name="sphere",
+            limit=58 if with_mass else 8,
+            scratch=[buffer(fixed.shape), buffer((2 * slots, 2 * columns, 256), jnp.bfloat16), signal, signal]
+            + [buffer((columns * slots, 128))] * 8,
         )
-        return exchange(done).reshape(spec_shape.shape)
-
-    def bind(body, *fixed):
-        return lambda *refs: body(*fixed, *refs)
-
-    table_high, table_low = call(
-        bind(legendre_body, degrees, devices, slots), (table_shape, table_shape), dev, jnp.asarray(place),
-        jnp.asarray(starts),
-        scratch=[pltpu.VMEM((slots, degrees), jnp.float32)] * 2 + [scratch128(degrees * slots)] * 2,
-        cost=pl.CostEstimate(flops=40_000_000, bytes_accessed=16 << 20, transcendentals=0), name="legendre",
-    )
+
+    def arrive(spec):
+        return exchange(spec).reshape(spec_shape.shape)
+
+    near, far = call(
+        bind(legendre_body, degrees, devices, slots), (near_shape, far_shape), fixed, far=(fixed,), far_out=(1,),
+        scratch=[buffer(fixed.shape)] + [buffer((slots, degrees))] * 2 + [buffer((degrees * slots, 128))] * 2
+        + [buffer(far_shape.shape, jnp.bfloat16), signal, signal],
+        cost=pl.CostEstimate(flops=40_000_000, bytes_accessed=16 << 20, transcendentals=0),
+        name="legendre", limit=60,
+    )
+    field = precip.reshape(rows, lon_total)
     flipped, spec = call(
-        bind(first_body, lat_rows), (grid_shape, spec_shape), dev, precip.reshape(rows, lon_total),
-        wave_high, wave_low, name="first",
-    )
+        bind(first_body, lat_rows), (grid_shape, spec_shape), field, wave, far=(field, wave), far_out=(0, 1),
+        name="first", limit=63,
+        scratch=[buffer((rows, lon_total)), buffer(wave.shape, jnp.bfloat16), buffer((rows, lon_total)),
+                 buffer(spec_shape.shape), pltpu.SemaphoreType.DMA((2 + 2 * QUART,))],
+    )
+    spec, far = sphere(spec, near, far, True)
     clamped, total, scaled = call(
-        bind(mass_body, lat_rows), (grid_shape, sum_shape, grid_shape), sphere(spec, True), flipped,
-        wave_high, wave_low, name="mass",
+        bind(mass_body, lat_rows), (grid_shape, sum_shape, grid_shape), arrive(spec), flipped, wave, name="mass",
     )
     count = float(members * fields)
     logs, spec = call(
-        bind(center_body, count, lat_rows), (grid_shape, spec_shape), clamped, total, swap(total),
-        wave_high, wave_low, name="center",
-    )
-    spec = call(ratio_body, spec_shape, sphere(spec, False), scaled, wave_high, wave_low, name="ratio")
+        bind(center_body, count, lat_rows), (grid_shape, spec_shape), clamped, total, swap(total), wave,
+        name="center",
+    )
+    spec = sphere(spec, near, far, False)
+    spec = call(ratio_body, spec_shape, arrive(spec), scaled, wave, name="ratio")
+    spec = sphere(spec, near, far, False)
     clamped, total = call(
-        bind(last_body, lat_rows), (grid_shape, sum_shape), dev, sphere(spec, False), logs, wave_high, wave_low,
-        scratch=[pltpu.VMEM((rows, lon_total), jnp.float32), pltpu.VMEM((lat_rows, lon_total), jnp.float32)],
-        name="last",
-    )
-    center = (total + swap(total)) / count
-    return jnp.exp(center), center[None] - clamped.reshape(precip.shape)
+        bind(last_body, lat_rows), (grid_shape, sum_shape), arrive(spec), logs, wave, name="last",
+    )
+    barycenter, logs = call(
+        bind(final_body, count, lat_rows), (sum_shape, grid_shape), clamped, total, swap(total), name="final",
+    )
+    return barycenter, logs.reshape(precip.shape)
 
 
 def fits_packed(mesh, shape):

time: 124 us -> 107 us (0.86)
  Pallas kernels: 34.5 us -> 26.2 us
  local copies, waits for them, and re-layouts: 8.8 us -> 2.09 us
  other arithmetic: 1.49 us -> 0 us
    pallas_call x9 -> x10, Pallas kernels: 34.5 us -> 26.2 us  [call(): pl.pallas_call(body, out_shape=shapes, in_specs=[hbm if any((o is f for f...]
    unnamed x26 -> x14, local copies, waits for them, and re-layouts: 8.8 us -> 2.09 us
  transfers between devices with their start and end apart: 3 -> 3, of which waited for: 3 -> 3; matrix products, arithmetic and copies ran while one was open for 0% -> 0% of each run, Pallas kernels for 5% -> 8%
where the time goes in v1:
time: 107 us
  blocking collectives  66 us (62%)
  Pallas kernels  26.2 us (24%)
  starting transfers between devices  7.45 us (7%)
  waiting for transfers between devices  4.34 us (4%)
  local copies, waits for them, and re-layouts  2.09 us (2%)
    all_to_all x5, blocking collectives, exchange(): lax.all_to_all(flat, ('lat', 'field'), split_axis=0, concat_axis=0, tiled...  66 us
    pallas_call x10, Pallas kernels, call(): pl.pallas_call(body, out_shape=shapes, in_specs=[hbm if any((o is f for f...  26.2 us
    all_to_all x1, starting transfers between devices, exchange(): lax.all_to_all(flat, ('lat', 'field'), split_axis=0, concat_axis=0, tiled...  7.3 us
    ppermute x2, waiting for transfers between devices, swap(): return lax.ppermute(value, 'field', [(0, 1), (1, 0)])  2.67 us
  transfers between devices with their start and end apart: 3, of which 3 were waited for; matrix products, arithmetic and copies ran while one was open for 0% of the time, Pallas kernels for 8%

profile of v1, /device:TPU:0, one launch (start us, length us, event | category | flops | bytes accessed | tf_op | source)
XLA Modules:
  0.0 106.9 jit_solution(4976736374234936614)
XLA Ops:
  0.6 3.3 %first.1 = (f32[64,1024]{1,0:T(8,128)}, f32[8,4,16,128]{3,2,1,0:T(8,128)}) custom-call(f32[64,1024]{1,0:T(8,128)} %bitcast.13, bf16[2,4,256,256]{3,2,1,0:T(8,128)(2,1)} %constant.5.clone.refs_1_.refs_2_.refs_3_.wave_ref), custom_call_target="tpu_custom_call" | custom-call | tf_op jit(solution)/shard_map/first/pallas_call | solution.py:604
  3.9 7.3 %all-to-all-start = ((f32[32,16,128]{2,1,0:T(8,128)}), f32[32,16,128]{2,1,0:T(8,128)S(1)}, u32[]{:S(2)}, u32[]{:S(2)}) async-start(f32[32,16,128]{2,1,0:T(8,128)} %bitcast.14), calls=%async_computation | async-start | bytes 524288 | tf_op jit(solution)/shard_map/all_to_all | solution.py:617
  11.2 8.9 %legendre.1 = (bf16[2,2912,256]{2,1,0:T(8,128)(2,1)}, bf16[2,1440,256]{2,1,0:T(8,128)(2,1)}) custom-call(f32[24,256]{1,0:T(8,128)} %constant.4.clone.refs_0_.refs_3_), custom_call_target="tpu_custom_call" | custom-call | flops 40000000 | bytes 16777216 | tf_op jit(solution)/shard_map/legendre/pallas_call | solution.py:604
  20.1 1.7 %all-to-all-done.refs_0_ = f32[32,16,128]{2,1,0:T(8,128)S(1)} async-done(((f32[32,16,128]{2,1,0:T(8,128)}), f32[32,16,128]{2,1,0:T(8,128)S(1)}, u32[]{:S(2)}, u32[]{:S(2)}) %all-to-all-start) | async-done | bytes 262176 | tf_op jit(solution)/shard_map/all_to_all | solution.py:617
  21.8 0.0 copy-start.6
  21.8 0.7 copy-done.6
  22.5 0.0 copy-start.1
  22.5 0.0 copy-start.4
  22.5 5.8 %sphere.3 = (f32[32,16,128]{2,1,0:T(8,128)}, bf16[2,1440,256]{2,1,0:T(8,128)(2,1)}) custom-call(f32[32,16,128]{2,1,0:T(8,128)} %copy-done.6, bf16[2,2912,256]{2,1,0:T(8,128)(2,1)} %get-tuple-element.18.refs_1_, bf16[2,1440,256]{2,1,0:T(8,128)(2,1)} %get-tuple-element.19.refs_2_, f32[24,256]{1,0:T(8,128)} %constant.4.clone.refs_0_.refs_3_), custom_call_target="tpu_custom_call" | custom-call | tf_op jit(solution)/shard_map/sphere/pallas_call | solution.py:604
  28.3 14.8 %all_to_all.30 = f32[32,16,128]{2,1,0:T(8,128)S(1)} all-to-all(f32[32,16,128]{2,1,0:T(8,128)} %get-tuple-element.20), channel_id=1, replica_groups=mesh['lat'=16,'field'=2] {'lat','field'}, dimensions={0} | all-to-all | bytes 524288 | tf_op jit(solution)/shard_map/all_to_all | solution.py:617
  43.1 0.0 copy-done.1
  43.1 0.0 copy-done.4
  43.1 0.5 mass.1
  43.6 0.1 collective-permute-start
  43.7 1.3 %collective-permute-done.refs_2_ = f32[32,1024]{1,0:T(8,128)S(1)} collective-permute-done((f32[32,1024]{1,0:T(8,128)S(1)}, f32[32,1024]{1,0:T(8,128)S(1)}, u32[]{:S(2)}, u32[]{:S(2)}) %collective-permute-start) | collective-permute-done | bytes 131104 | tf_op jit(solution)/shard_map/ppermute | solution.py:620
  45.0 0.6 center.1
  45.6 12.8 %all_to_all.31.refs_0_ = f32[32,16,128]{2,1,0:T(8,128)S(1)} all-to-all(f32[32,16,128]{2,1,0:T(8,128)S(1)} %bitcast.12), channel_id=1, replica_groups=mesh['lat'=16,'field'=2] {'lat','field'}, dimensions={0} | all-to-all | bytes 524288 | tf_op jit(solution)/shard_map/all_to_all | solution.py:617
  58.4 0.0 copy-done
  58.4 0.0 copy-done.5
  58.4 1.4 %copy-done.2 = bf16[2,1440,256]{2,1,0:T(8,128)(2,1)S(1)} copy-done((bf16[2,1440,256]{2,1,0:T(8,128)(2,1)S(1)}, bf16[2,1440,256]{2,1,0:T(8,128)(2,1)}, u32[]{:S(2)}) %copy-start.2) | copy-done | bytes 1474584
  59.8 2.5 %sphere.4 = f32[32,16,128]{2,1,0:T(8,128)S(1)} custom-call(f32[32,16,128]{2,1,0:T(8,128)S(1)} %all_to_all.31.refs_0_, bf16[2,2912,256]{2,1,0:T(8,128)(2,1)S(1)} %copy-done, bf16[2,1440,256]{2,1,0:T(8,128)(2,1)S(1)} %copy-done.2, f32[24,256]{1,0:T(8,128)S(1)} %copy-done.5), custom_call_target="tpu_custom_call" | custom-call | tf_op jit(solution)/shard_map/sphere/pallas_call | solution.py:604
  62.3 0.0 copy-start.3
  62.3 12.8 %all_to_all.32 = f32[32,16,128]{2,1,0:T(8,128)S(1)} all-to-all(f32[32,16,128]{2,1,0:T(8,128)S(1)} %sphere.4), channel_id=1, replica_groups=mesh['lat'=16,'field'=2] {'lat','field'}, dimensions={0} | all-to-all | bytes 524288 | tf_op jit(solution)/shard_map/all_to_all | solution.py:617
  75.1 1.0 ratio.1
  76.1 12.8 %all_to_all.33.refs_0_ = f32[32,16,128]{2,1,0:T(8,128)S(1)} all-to-all(f32[32,16,128]{2,1,0:T(8,128)S(1)} %bitcast.9), channel_id=1, replica_groups=mesh['lat'=16,'field'=2] {'lat','field'}, dimensions={0} | all-to-all | bytes 524288 | tf_op jit(solution)/shard_map/all_to_all | solution.py:617
  88.9 0.0 copy-done.3
  88.9 2.5 %sphere.5 = f32[32,16,128]{2,1,0:T(8,128)S(1)} custom-call(f32[32,16,128]{2,1,0:T(8,128)S(1)} %all_to_all.33.refs_0_, bf16[2,2912,256]{2,1,0:T(8,128)(2,1)S(1)} %copy-done, bf16[2,1440,256]{2,1,0:T(8,128)(2,1)S(1)} %copy-done.3, f32[24,256]{1,0:T(8,128)S(1)} %copy-done.5), custom_call_target="tpu_custom_call" | custom-call | tf_op jit(solution)/shard_map/sphere/pallas_call | solution.py:604
  91.4 12.8 %all_to_all.34 = f32[32,16,128]{2,1,0:T(8,128)S(1)} all-to-all(f32[32,16,128]{2,1,0:T(8,128)S(1)} %sphere.5), channel_id=1, replica_groups=mesh['lat'=16,'field'=2] {'lat','field'}, dimensions={0} | all-to-all | bytes 524288 | tf_op jit(solution)/shard_map/all_to_all | solution.py:617
  104.2 0.5 last.1
  104.7 0.1 collective-permute-start.1
  104.8 1.3 %collective-permute-done.1.refs_2_ = f32[32,1024]{1,0:T(8,128)S(1)} collective-permute-done((f32[32,1024]{1,0:T(8,128)S(1)}, f32[32,1024]{1,0:T(8,128)S(1)}, u32[]{:S(2)}, u32[]{:S(2)}) %collective-permute-start.1) | collective-permute-done | bytes 131104 | tf_op jit(solution)/shard_map/ppermute | solution.py:620
  106.1 0.8 final.1
  (3 shorter events, 0.0 us)
Async XLA Ops:
  3.9 17.9 %all-to-all-start = ((f32[32,16,128]{2,1,0:T(8,128)}), f32[32,16,128]{2,1,0:T(8,128)S(1)}, u32[]{:S(2)}, u32[]{:S(2)}) async-start(f32[32,16,128]{2,1,0:T(8,128)} %bitcast.14), calls=%async_computation | async-start | bytes 524288 | tf_op jit(solution)/shard_map/all_to_all | solution.py:617
  21.8 0.7 copy-start.6
  22.5 20.6 %copy-start.1 = (bf16[2,4,256,256]{3,2,1,0:T(8,128)(2,1)S(1)}, bf16[2,4,256,256]{3,2,1,0:T(8,128)(2,1)}, u32[]{:S(2)}) copy-start(bf16[2,4,256,256]{3,2,1,0:T(8,128)(2,1)} %constant.5.clone.refs_1_.refs_2_.refs_3_.wave_ref) | copy-start | bytes 3145732
  22.5 20.6 %copy-start.4 = (f32[64,1024]{1,0:T(8,128)S(1)}, f32[64,1024]{1,0:T(8,128)}, u32[]{:S(2)}) copy-start(f32[64,1024]{1,0:T(8,128)} %get-tuple-element.21.refs_1_) | copy-start | bytes 786436
  43.1 15.3 %copy-start = (bf16[2,2912,256]{2,1,0:T(8,128)(2,1)S(1)}, bf16[2,2912,256]{2,1,0:T(8,128)(2,1)}, u32[]{:S(2)}) copy-start(bf16[2,2912,256]{2,1,0:T(8,128)(2,1)} %get-tuple-element.18.refs_1_) | copy-start | bytes 8945668
  43.1 15.3 %copy-start.5 = (f32[24,256]{1,0:T(8,128)S(1)}, f32[24,256]{1,0:T(8,128)}, u32[]{:S(2)}) copy-start(f32[24,256]{1,0:T(8,128)} %constant.4.clone.refs_0_.refs_3_) | copy-start | bytes 73732
  43.6 1.4 %collective-permute-start = (f32[32,1024]{1,0:T(8,128)S(1)}, f32[32,1024]{1,0:T(8,128)S(1)}, u32[]{:S(2)}, u32[]{:S(2)}) collective-permute-start(f32[32,1024]{1,0:T(8,128)S(1)} %get-tuple-element.23.refs_1_), channel_id=1, source_target_pairs={{0,1},{1,0},{2,3},{3,2},{4,5},{5,4},{6,7},{7,6},{8,9},{9,8},{10,11... | collective-permute-start | bytes 393224 | tf_op jit(solution)/shard_map/ppermute | solution.py:620
  58.4 1.4 %copy-start.2 = (bf16[2,1440,256]{2,1,0:T(8,128)(2,1)S(1)}, bf16[2,1440,256]{2,1,0:T(8,128)(2,1)}, u32[]{:S(2)}) copy-start(bf16[2,1440,256]{2,1,0:T(8,128)(2,1)} %get-tuple-element.25.refs_2_) | copy-start | bytes 4423684
  62.3 26.6 %copy-start.3 = (bf16[2,1440,256]{2,1,0:T(8,128)(2,1)S(1)}, bf16[2,1440,256]{2,1,0:T(8,128)(2,1)}, u32[]{:S(2)}) copy-start(bf16[2,1440,256]{2,1,0:T(8,128)(2,1)} %get-tuple-element.25.refs_2_) | copy-start | bytes 4423684
  104.7 1.4 %collective-permute-start.1 = (f32[32,1024]{1,0:T(8,128)S(1)}, f32[32,1024]{1,0:T(8,128)S(1)}, u32[]{:S(2)}, u32[]{:S(2)}) collective-permute-start(f32[32,1024]{1,0:T(8,128)S(1)} %get-tuple-element.29.refs_1_), channel_id=1, source_target_pairs={{0,1},{1,0},{2,3},{3,2},{4,5},{5,4},{6,7},{7,6},{8,9},{9,8},{10,11... | collective-permute-start | bytes 393224 | tf_op jit(solution)/shard_map/ppermute | solution.py:620

commit v2 on v1

--- a/solution.py
+++ b/solution.py
@@ -502,12 +502,10 @@
 
 
 def sphere_body(degrees, devices, slots, lat_groups, lat_rows, members, with_mass, spec_ref, near_ref, far_in,
-                fixed_hbm, out_ref, *rest):
+                fixed_ref, out_ref, *rest):
     far_ref, rest = (rest[0], rest[1:]) if with_mass else (far_in, rest)
-    fixed_ref, coef_ref, sem, far_sem = rest[:4]
-    halves = rest[4:]
-    copy = pltpu.make_async_copy(fixed_hbm, fixed_ref, sem)
-    copy.start()
+    coef_ref, far_sem = rest[:2]
+    halves = rest[2:]
     if with_mass:
         get_far = pltpu.make_async_copy(far_in, far_ref, far_sem)
         get_far.start()
@@ -518,7 +516,6 @@
     per_field = 2 * members
     columns = fields * per_field
     gather_orders(spec_ref, sign, fields, lat_groups, lat_rows, per_field, slots, even_in, odd_in)
-    copy.wait()
     mass = None
 
     def pick(slot, parity):
@@ -600,11 +597,19 @@
 
     def call(body, shapes, *operands, name, far=(), far_out=(), scratch=(), cost=None, limit=8):
         single = not isinstance(shapes, tuple)
-        outs = [hbm if index in far_out else vmem for index in range(1 if single else len(shapes))]
+        shapes = (shapes,) if single else shapes
+        outs = [hbm if index in far_out else vmem for index in range(len(shapes))]
+        shapes = [
+            pltpu.HBM(shape.shape, shape.dtype) if index in far_out else shape for index, shape in enumerate(shapes)
+        ]
+        specs = [hbm if any(o is f for f in far) else vmem for o in operands]
+        operands = [
+            pltpu.with_memory_space_constraint(o, pltpu.HBM) if any(o is f for f in far) else o for o in operands
+        ]
         return pl.pallas_call(
             body,
-            out_shape=shapes,
-            in_specs=[hbm if any(o is f for f in far) else vmem for o in operands],
+            out_shape=shapes[0] if single else shapes,
+            in_specs=specs,
             out_specs=outs[0] if single else outs,
             scratch_shapes=list(scratch),
             cost_estimate=cost,
@@ -632,9 +637,9 @@
         return call(
             bind(sphere_body, degrees, devices, slots, lat_groups, lat_rows, members, with_mass),
             (flat_shape, far_shape) if with_mass else flat_shape,
-            exchange(spec), near, far, fixed, far=(far, fixed) if with_mass else (fixed,), name="sphere",
-            limit=58 if with_mass else 8,
-            scratch=[buffer(fixed.shape), buffer((2 * slots, 2 * columns, 256), jnp.bfloat16), signal, signal]
+            exchange(spec), near, far, fixed, far=(far,) if with_mass else (), name="sphere",
+            limit=8,
+            scratch=[buffer((2 * slots, 2 * columns, 256), jnp.bfloat16), signal]
             + [buffer((columns * slots, 128))] * 8,
         )
 
@@ -646,12 +651,12 @@
         scratch=[buffer(fixed.shape)] + [buffer((slots, degrees))] * 2 + [buffer((degrees * slots, 128))] * 2
         + [buffer(far_shape.shape, jnp.bfloat16), signal, signal],
         cost=pl.CostEstimate(flops=40_000_000, bytes_accessed=16 << 20, transcendentals=0),
-        name="legendre", limit=60,
+        name="legendre", limit=12,
     )
     field = precip.reshape(rows, lon_total)
     flipped, spec = call(
         bind(first_body, lat_rows), (grid_shape, spec_shape), field, wave, far=(field, wave), far_out=(0, 1),
-        name="first", limit=63,
+        name="first", limit=8,
         scratch=[buffer((rows, lon_total)), buffer(wave.shape, jnp.bfloat16), buffer((rows, lon_total)),
                  buffer(spec_shape.shape), pltpu.SemaphoreType.DMA((2 + 2 * QUART,))],
     )

time: 107 us -> 100 us (0.935)
  Pallas kernels: 26.2 us -> 21.4 us
  local copies, waits for them, and re-layouts: 2.09 us -> 0.01 us
  blocking collectives: 66 us -> 64.2 us
  waiting for transfers between devices: 4.34 us -> 5.96 us
    pallas_call x10, Pallas kernels: 26.2 us -> 21.4 us  [call(): pl.pallas_call(body, out_shape=shapes[0] if single else shapes, in_specs=...]
    unnamed x14 -> x6, local copies, waits for them, and re-layouts: 2.09 us -> 0.01 us
    all_to_all x5, blocking collectives: 66 us -> 64.2 us  [exchange(): lax.all_to_all(flat, ('lat', 'field'), split_axis=0, concat_axis=0, tiled...]
    all_to_all x1, waiting for transfers between devices: 1.67 us -> 3.29 us  [exchange(): lax.all_to_all(flat, ('lat', 'field'), split_axis=0, concat_axis=0, tiled...]
  transfers between devices with their start and end apart: 3 -> 3, of which waited for: 3 -> 3; matrix products, arithmetic and copies ran while one was open for 0% -> 0% of each run, Pallas kernels for 8% -> 7%
where the time goes in v2:
time: 100 us; the launch traced here: 99.8 us
  blocking collectives  64.2 us (64%)
  Pallas kernels  21.4 us (21%)
  starting transfers between devices  7.45 us (7%)
  waiting for transfers between devices  5.96 us (6%)
    all_to_all x5, blocking collectives, exchange(): lax.all_to_all(flat, ('lat', 'field'), split_axis=0, concat_axis=0, tiled...  64.2 us
    pallas_call x10, Pallas kernels, call(): pl.pallas_call(body, out_shape=shapes[0] if single else shapes, in_specs=...  21.4 us
    all_to_all x1, starting transfers between devices, exchange(): lax.all_to_all(flat, ('lat', 'field'), split_axis=0, concat_axis=0, tiled...  7.3 us
    all_to_all x1, waiting for transfers between devices, exchange(): lax.all_to_all(flat, ('lat', 'field'), split_axis=0, concat_axis=0, tiled...  3.29 us
    ppermute x2, waiting for transfers between devices, swap(): return lax.ppermute(value, 'field', [(0, 1), (1, 0)])  2.67 us
  transfers between devices with their start and end apart: 3, of which 3 were waited for; matrix products, arithmetic and copies ran while one was open for 0% of the time, Pallas kernels for 7%

profile of v2, /device:TPU:0, one launch (start us, length us, event | category | flops | bytes accessed | tf_op | source)
XLA Modules:
  0.0 99.8 jit_solution(3552317075204739679)
XLA Ops:
  0.6 0.0 copy-start.2
  0.6 3.3 %first.1 = (f32[64,1024]{1,0:T(8,128)}, f32[8,4,16,128]{3,2,1,0:T(8,128)}) custom-call(f32[64,1024]{1,0:T(8,128)} %bitcast.13, bf16[2,4,256,256]{3,2,1,0:T(8,128)(2,1)} %constant.5.clone.refs_1_.refs_2_.refs_3_.wave_ref), custom_call_target="tpu_custom_call" | custom-call | tf_op jit(solution)/shard_map/first/pallas_call | solution.py:609
  3.9 7.3 %all-to-all-start = ((f32[32,16,128]{2,1,0:T(8,128)}), f32[32,16,128]{2,1,0:T(8,128)S(1)}, u32[]{:S(2)}, u32[]{:S(2)}) async-start(f32[32,16,128]{2,1,0:T(8,128)} %bitcast.14), calls=%async_computation | async-start | bytes 524288 | tf_op jit(solution)/shard_map/all_to_all | solution.py:622
  11.2 7.3 %legendre.1 = (bf16[2,2912,256]{2,1,0:T(8,128)(2,1)S(1)}, bf16[2,1440,256]{2,1,0:T(8,128)(2,1)}) custom-call(f32[24,256]{1,0:T(8,128)} %constant.4.clone.refs_0_.refs_3_), custom_call_target="tpu_custom_call" | custom-call | flops 40000000 | bytes 16777216 | tf_op jit(solution)/shard_map/legendre/pallas_call | solution.py:609
  18.5 3.3 %all-to-all-done.refs_0_ = f32[32,16,128]{2,1,0:T(8,128)S(1)} async-done(((f32[32,16,128]{2,1,0:T(8,128)}), f32[32,16,128]{2,1,0:T(8,128)S(1)}, u32[]{:S(2)}, u32[]{:S(2)}) %all-to-all-start) | async-done | bytes 262176 | tf_op jit(solution)/shard_map/all_to_all | solution.py:622
  21.8 0.0 copy-done.2
  21.8 0.0 copy-start
  21.8 0.0 copy-start.1
  21.8 2.9 %sphere.3 = (f32[32,16,128]{2,1,0:T(8,128)S(1)}, bf16[2,1440,256]{2,1,0:T(8,128)(2,1)S(1)}) custom-call(f32[32,16,128]{2,1,0:T(8,128)S(1)} %all-to-all-done.refs_0_, bf16[2,2912,256]{2,1,0:T(8,128)(2,1)S(1)} %get-tuple-element.18.refs_1_, bf16[2,1440,256]{2,1,0:T(8,128)(2,1)} %get-tuple-element.19.refs_2_, f32[24,256]{1,0:T(8,128)S(1)} %copy-done.2), custom_call_target="tpu_custom_call" | custom-call | tf_op jit(solution)/shard_map/sphere/pallas_call | solution.py:609
  24.7 13.0 %all_to_all.30 = f32[32,16,128]{2,1,0:T(8,128)S(1)} all-to-all(f32[32,16,128]{2,1,0:T(8,128)S(1)} %get-tuple-element.20), channel_id=1, replica_groups=mesh['lat'=16,'field'=2] {'lat','field'}, dimensions={0} | all-to-all | bytes 524288 | tf_op jit(solution)/shard_map/all_to_all | solution.py:622
  37.7 0.0 copy-done
  37.7 0.0 copy-done.1
  37.7 0.5 mass.1
  38.2 0.1 collective-permute-start
  38.3 1.3 %collective-permute-done.refs_2_ = f32[32,1024]{1,0:T(8,128)S(1)} collective-permute-done((f32[32,1024]{1,0:T(8,128)S(1)}, f32[32,1024]{1,0:T(8,128)S(1)}, u32[]{:S(2)}, u32[]{:S(2)}) %collective-permute-start) | collective-permute-done | bytes 131104 | tf_op jit(solution)/shard_map/ppermute | solution.py:625
  39.6 0.6 center.1
  40.2 12.8 %all_to_all.31.refs_0_ = f32[32,16,128]{2,1,0:T(8,128)S(1)} all-to-all(f32[32,16,128]{2,1,0:T(8,128)S(1)} %bitcast.12), channel_id=1, replica_groups=mesh['lat'=16,'field'=2] {'lat','field'}, dimensions={0} | all-to-all | bytes 524288 | tf_op jit(solution)/shard_map/all_to_all | solution.py:622
  53.0 2.3 %sphere.4 = f32[32,16,128]{2,1,0:T(8,128)S(1)} custom-call(f32[32,16,128]{2,1,0:T(8,128)S(1)} %all_to_all.31.refs_0_, bf16[2,2912,256]{2,1,0:T(8,128)(2,1)S(1)} %get-tuple-element.18.refs_1_, bf16[2,1440,256]{2,1,0:T(8,128)(2,1)S(1)} %get-tuple-element.25.refs_2_, f32[24,256]{1,0:T(8,128)S(1)} %copy-done.2), custom_call_target="tpu_custom_call" | custom-call | tf_op jit(solution)/shard_map/sphere/pallas_call | solution.py:609
  55.4 12.8 %all_to_all.32 = f32[32,16,128]{2,1,0:T(8,128)S(1)} all-to-all(f32[32,16,128]{2,1,0:T(8,128)S(1)} %sphere.4), channel_id=1, replica_groups=mesh['lat'=16,'field'=2] {'lat','field'}, dimensions={0} | all-to-all | bytes 524288 | tf_op jit(solution)/shard_map/all_to_all | solution.py:622
  68.2 1.0 ratio.1
  69.2 12.8 %all_to_all.33.refs_0_ = f32[32,16,128]{2,1,0:T(8,128)S(1)} all-to-all(f32[32,16,128]{2,1,0:T(8,128)S(1)} %bitcast.9), channel_id=1, replica_groups=mesh['lat'=16,'field'=2] {'lat','field'}, dimensions={0} | all-to-all | bytes 524288 | tf_op jit(solution)/shard_map/all_to_all | solution.py:622
  82.0 2.3 %sphere.5 = f32[32,16,128]{2,1,0:T(8,128)S(1)} custom-call(f32[32,16,128]{2,1,0:T(8,128)S(1)} %all_to_all.33.refs_0_, bf16[2,2912,256]{2,1,0:T(8,128)(2,1)S(1)} %get-tuple-element.18.refs_1_, bf16[2,1440,256]{2,1,0:T(8,128)(2,1)S(1)} %get-tuple-element.25.refs_2_, f32[24,256]{1,0:T(8,128)S(1)} %copy-done.2), custom_call_target="tpu_custom_call" | custom-call | tf_op jit(solution)/shard_map/sphere/pallas_call | solution.py:609
  84.3 12.8 %all_to_all.34 = f32[32,16,128]{2,1,0:T(8,128)S(1)} all-to-all(f32[32,16,128]{2,1,0:T(8,128)S(1)} %sphere.5), channel_id=1, replica_groups=mesh['lat'=16,'field'=2] {'lat','field'}, dimensions={0} | all-to-all | bytes 524288 | tf_op jit(solution)/shard_map/all_to_all | solution.py:622
  97.1 0.5 last.1
  97.6 0.1 collective-permute-start.1
  97.7 1.3 %collective-permute-done.1.refs_2_ = f32[32,1024]{1,0:T(8,128)S(1)} collective-permute-done((f32[32,1024]{1,0:T(8,128)S(1)}, f32[32,1024]{1,0:T(8,128)S(1)}, u32[]{:S(2)}, u32[]{:S(2)}) %collective-permute-start.1) | collective-permute-done | bytes 131104 | tf_op jit(solution)/shard_map/ppermute | solution.py:625
  99.0 0.8 final.1
Async XLA Ops:
  0.6 21.2 %copy-start.2 = (f32[24,256]{1,0:T(8,128)S(1)}, f32[24,256]{1,0:T(8,128)}, u32[]{:S(2)}) copy-start(f32[24,256]{1,0:T(8,128)} %constant.4.clone.refs_0_.refs_3_) | copy-start | bytes 73732
  3.9 17.9 %all-to-all-start = ((f32[32,16,128]{2,1,0:T(8,128)}), f32[32,16,128]{2,1,0:T(8,128)S(1)}, u32[]{:S(2)}, u32[]{:S(2)}) async-start(f32[32,16,128]{2,1,0:T(8,128)} %bitcast.14), calls=%async_computation | async-start | bytes 524288 | tf_op jit(solution)/shard_map/all_to_all | solution.py:622
  21.8 15.9 %copy-start = (bf16[2,4,256,256]{3,2,1,0:T(8,128)(2,1)S(1)}, bf16[2,4,256,256]{3,2,1,0:T(8,128)(2,1)}, u32[]{:S(2)}) copy-start(bf16[2,4,256,256]{3,2,1,0:T(8,128)(2,1)} %constant.5.clone.refs_1_.refs_2_.refs_3_.wave_ref) | copy-start | bytes 3145732
  21.8 15.9 %copy-start.1 = (f32[64,1024]{1,0:T(8,128)S(1)}, f32[64,1024]{1,0:T(8,128)}, u32[]{:S(2)}) copy-start(f32[64,1024]{1,0:T(8,128)} %get-tuple-element.21.refs_1_) | copy-start | bytes 786436
  38.2 1.4 %collective-permute-start = (f32[32,1024]{1,0:T(8,128)S(1)}, f32[32,1024]{1,0:T(8,128)S(1)}, u32[]{:S(2)}, u32[]{:S(2)}) collective-permute-start(f32[32,1024]{1,0:T(8,128)S(1)} %get-tuple-element.23.refs_1_), channel_id=1, source_target_pairs={{0,1},{1,0},{2,3},{3,2},{4,5},{5,4},{6,7},{7,6},{8,9},{9,8},{10,11... | collective-permute-start | bytes 393224 | tf_op jit(solution)/shard_map/ppermute | solution.py:625
  97.6 1.4 %collective-permute-start.1 = (f32[32,1024]{1,0:T(8,128)S(1)}, f32[32,1024]{1,0:T(8,128)S(1)}, u32[]{:S(2)}, u32[]{:S(2)}) collective-permute-start(f32[32,1024]{1,0:T(8,128)S(1)} %get-tuple-element.29.refs_1_), channel_id=1, source_target_pairs={{0,1},{1,0},{2,3},{3,2},{4,5},{5,4},{6,7},{7,6},{8,9},{9,8},{10,11... | collective-permute-start | bytes 393224 | tf_op jit(solution)/shard_map/ppermute | solution.py:625

commit v3 on v2

--- a/solution.py
+++ b/solution.py
@@ -215,7 +215,33 @@
     return np.stack([high, low])
 
 
-def forward_waves(field, wave_ref, out_ref, ready=None, done=None):
+def wave_seeds(lon_total, devices, slots):
+    span = lon_total // QUART
+    first = (np.arange(QUART)[:, None] + QUART * np.arange(devices // QUART)[None, :]).reshape(-1)
+    phases = [
+        orders[:, None] * np.arange(span)[None, :] % lon_total * (2.0 * np.pi / lon_total)
+        for orders in (first, devices * np.arange(slots))
+    ]
+    return np.concatenate([f(p) for p in phases for f in (np.cos, np.sin)]).astype(np.float32)
+
+
+def grow_waves(seed_ref, wave_ref, devices, slots):
+    orders = wave_ref.shape[2] // 2
+    step_cos = seed_ref[2 * devices : 2 * devices + slots, :]
+    step_sin = seed_ref[2 * devices + slots : 2 * devices + 2 * slots, :]
+    for row in range(devices):
+        residue, at = row // (devices // QUART), row % (devices // QUART) * slots
+        cosine, sine = seed_ref[row : row + 1, :], seed_ref[devices + row : devices + row + 1, :]
+        for place, value in (
+            (at, cosine * step_cos - sine * step_sin),
+            (orders + at, sine * step_cos + cosine * step_sin),
+        ):
+            high, low = split_pair(value)
+            wave_ref[0, residue, place : place + slots, :] = high
+            wave_ref[1, residue, place : place + slots, :] = low
+
+
+def forward_waves(field, wave_ref, out_ref, done=None):
     span = field.shape[1] // QUART
     rows = field.shape[0]
     lanes = 2 * rows
@@ -228,8 +254,6 @@
     first = lax.broadcasted_iota(jnp.int32, (orders, lanes), 1) < rows
     for residue in range(QUART):
         stack = stack_odd if residue % 2 else stack_even
-        if ready:
-            ready[residue].wait()
         found = dot_nt(wave_ref[0, residue], stack) + dot_nt(wave_ref[1, residue], stack)
         found = found[:, :lanes] + found[:, lanes:]
         cosine, sine = found[:orders], found[orders:]
@@ -300,22 +324,22 @@
     return lax.axis_index("lat") >= lax.axis_size("lat") // 2
 
 
-def first_body(lat_rows, field_hbm, wave_hbm, flipped_hbm, out_hbm, field_ref, wave_ref, flipped_ref, out_ref, sems):
+def first_body(lat_rows, devices, slots, field_hbm, seed_hbm, flipped_hbm, out_hbm, field_ref, seed_ref, wave_ref,
+               flipped_ref, out_ref, sems):
     get_field = pltpu.make_async_copy(field_hbm, field_ref, sems.at[0])
-    get_wave = [
-        pltpu.make_async_copy(wave_hbm.at[:, r], wave_ref.at[:, r], sems.at[1 + r]) for r in range(QUART)
+    get_seed = pltpu.make_async_copy(seed_hbm, seed_ref, sems.at[1])
+    put_flipped = pltpu.make_async_copy(flipped_ref, flipped_hbm, sems.at[2])
+    put_wave = [
+        pltpu.make_async_copy(out_ref.at[:, r], out_hbm.at[:, r], sems.at[3 + r]) for r in range(QUART)
     ]
-    put_flipped = pltpu.make_async_copy(flipped_ref, flipped_hbm, sems.at[1 + QUART])
-    put_wave = [
-        pltpu.make_async_copy(out_ref.at[:, r], out_hbm.at[:, r], sems.at[2 + QUART + r]) for r in range(QUART)
-    ]
+    get_seed.start()
     get_field.start()
-    for copy in get_wave:
-        copy.start()
+    get_seed.wait()
+    grow_waves(seed_ref, wave_ref, devices, slots)
     get_field.wait()
     flipped_ref[...] = flip_rows(field_ref[...], in_south(), lat_rows)
     put_flipped.start()
-    forward_waves(flipped_ref[...], wave_ref, out_ref, get_wave, put_wave)
+    forward_waves(flipped_ref[...], wave_ref, out_ref, put_wave)
     put_flipped.wait()
     for copy in put_wave:
         copy.wait()
@@ -328,41 +352,50 @@
     return total
 
 
-def mass_body(lat_rows, spec_ref, field_ref, wave_ref, clamp_ref, sum_ref, scaled_ref):
+def core_select(core, first, second):
+    return jnp.where(core == 0, first, second), jnp.where(core == 0, second, first)
+
+
+def center_body(count, part_rows, spec_ref, wave_ref, logs_ref, inverse_ref, out_ref):
     blurred, total = inverse_waves(spec_ref, wave_ref)
     inverse = (4.0 * math.pi) / total
-    scaled_ref[...] = field_ref[...] * inverse
     clamped = jnp.log(jnp.maximum(blurred * inverse, floor_value))
-    clamp_ref[...] = clamped
-    sum_ref[...] = member_sum(clamped, lat_rows)
-
-
-def center_body(count, lat_rows, clamp_ref, sum_ref, other_ref, wave_ref, logs_ref, out_ref):
-    center = (sum_ref[...] + other_ref[...]) / count
-    members = clamp_ref.shape[0] // lat_rows
-    logs = jnp.concatenate([center] * members, axis=0) - clamp_ref[...]
+    center = member_sum(clamped, part_rows) / count
+    logs = jnp.concatenate([center] * (clamped.shape[0] // part_rows), axis=0) - clamped
     logs_ref[...] = logs
     forward_waves(jnp.exp(logs), wave_ref, out_ref)
-
-
-def ratio_body(spec_ref, scaled_ref, wave_ref, out_ref):
+    half = inverse.shape[0] // 2
+    own, _ = core_select(lax.axis_index("field"), inverse[:half], inverse[half:])
+    parts = [own[at : at + part_rows] for at in range(0, half, part_rows)]
+    inverse_ref[...] = jnp.broadcast_to(jnp.concatenate([p for p in parts for _ in range(2)], axis=0), inverse_ref.shape)
+
+
+def ratio_body(spec_ref, field_ref, inverse_ref, wave_ref, out_ref):
     blurred, _ = inverse_waves(spec_ref, wave_ref)
-    forward_waves(scaled_ref[...] / jnp.maximum(blurred, floor_value), wave_ref, out_ref)
-
-
-def last_body(lat_rows, spec_ref, logs_ref, wave_ref, clamp_ref, sum_ref):
+    scaled = field_ref[...] * inverse_ref[:, 0:1]
+    forward_waves(scaled / jnp.maximum(blurred, floor_value), wave_ref, out_ref)
+
+
+def last_body(count, part_rows, spec_ref, logs_ref, wave_ref, keep_ref, send_ref):
     blurred, _ = inverse_waves(spec_ref, wave_ref)
     clamped = jnp.log(jnp.maximum(blurred, floor_value))
-    clamp_ref[...] = clamped
-    sum_ref[...] = member_sum(logs_ref[...] + clamped, lat_rows)
-
-
-def final_body(count, lat_rows, clamp_ref, sum_ref, other_ref, center_ref, logs_ref):
-    south = in_south()
-    center = flip_rows((sum_ref[...] + other_ref[...]) / count, south, lat_rows)
-    center_ref[...] = jnp.exp(center)
-    members = clamp_ref.shape[0] // lat_rows
-    logs_ref[...] = jnp.concatenate([center] * members, axis=0) - flip_rows(clamp_ref[...], south, lat_rows)
+    center = member_sum(logs_ref[...] + clamped, part_rows) / count
+    logs = jnp.concatenate([center] * (clamped.shape[0] // part_rows), axis=0) - clamped
+    half = logs.shape[0] // 2
+    own, other = core_select(lax.axis_index("field"), logs[:half], logs[half:])
+    keep_ref[...] = jnp.concatenate([own, center], axis=0)
+    send_ref[...] = jnp.concatenate([other, center], axis=0)
+
+
+def final_body(part_rows, keep_ref, got_ref, center_ref, logs_ref):
+    low, high = core_select(lax.axis_index("field"), keep_ref[...], got_ref[...])
+    pieces = []
+    for at in range(0, low.shape[0], part_rows):
+        pieces += [low[at : at + part_rows], high[at : at + part_rows]]
+    whole = flip_rows(jnp.concatenate(pieces, axis=0), in_south(), 2 * part_rows)
+    rows = logs_ref.shape[0]
+    logs_ref[...] = whole[:rows]
+    center_ref[...] = jnp.exp(whole[rows:])
 
 
 def table_rows(degrees, devices, slot):
@@ -385,8 +418,13 @@
     return near_ref, offset - table_offset(degrees, devices, FAR_SLOTS, 0), count
 
 
-def legendre_body(degrees, devices, slots, fixed_hbm, near_ref, far_hbm, fixed_ref, first_coef,
-                  second_coef, left_half, right_half, far_ref, sem, far_sem):
+def move_far(degrees, devices, slot, src_ref, dst_ref, sems):
+    part = (slice(None), pl.ds(table_offset(degrees, devices, slot, 0), 2 * table_rows(degrees, devices, slot)))
+    return pltpu.make_async_copy(src_ref.at[part], dst_ref.at[part], sems.at[slot])
+
+
+def legendre_body(degrees, devices, slots, fixed_hbm, near_ref, far_hbm, weight_ref, fixed_ref, first_coef,
+                  second_coef, left_half, right_half, far_ref, sem, far_sems):
     copy = pltpu.make_async_copy(fixed_hbm, fixed_ref, sem)
     copy.start()
     half = (left_half, right_half)
@@ -456,7 +494,7 @@
             states.append(fresh(len(states)))
         states = chunk(index, states)
 
-    put_far = pltpu.make_async_copy(far_ref, far_hbm, far_sem)
+    weight_ref[...] = fixed_ref[slots + 2 : slots + 3, :]
     for slot in range(slots):
         for parity in range(2):
             part_ref, offset, count = table_part(degrees, devices, slot, parity, near_ref, far_ref)
@@ -465,44 +503,60 @@
                 high, low = split_pair(half[h][pl.ds(begin, count, stride=2 * slots), :])
                 part_ref[0, offset : offset + count, h * lanes : (h + 1) * lanes] = high
                 part_ref[1, offset : offset + count, h * lanes : (h + 1) * lanes] = low
-        if slot == FAR_SLOTS - 1:
-            put_far.start()
-    put_far.wait()
-
-
-def gather_orders(spec_ref, sign, fields, lat_groups, lat_rows, per_field, slots, even_in, odd_in):
+        if slot < FAR_SLOTS:
+            move_far(degrees, devices, slot, far_ref, far_hbm, far_sems).start()
+    for slot in range(FAR_SLOTS):
+        move_far(degrees, devices, slot, far_ref, far_hbm, far_sems).wait()
+
+
+def gather_orders(spec_ref, sign, fields, lat_groups, lat_rows, members, slots, halved, even_in, odd_in):
     group_lanes = 128 // lat_rows
-    for field in range(fields):
-        for h in range(2):
-            even, odd = [], []
-            for q in range(group_lanes):
+    width = lat_rows // fields if halved else lat_rows
+    for h in range(2):
+        even, odd = {}, {}
+        for q in range(group_lanes):
+            for source in range(fields):
                 lat = h * group_lanes + q
-                north = spec_ref[lat * fields + field]
-                south = spec_ref[(lat_groups - 1 - lat) * fields + field] * sign
-                even.append(north + south)
-                odd.append(north - south)
-            for c in range(per_field):
-                row = (field * per_field + c) * slots
-                cut = slice(c * lat_rows, (c + 1) * lat_rows)
-                even_in[h][row : row + slots, :] = jnp.concatenate([e[:, cut] for e in even], axis=1)
-                odd_in[h][row : row + slots, :] = jnp.concatenate([o[:, cut] for o in odd], axis=1)
-
-
-def scatter_orders(out_ref, fields, lat_groups, lat_rows, per_field, slots, north, south):
+                north = spec_ref[lat * fields + source]
+                south = spec_ref[(lat_groups - 1 - lat) * fields + source] * sign
+                even[q, source] = north + south
+                odd[q, source] = north - south
+        for field in range(fields):
+            for c in range(2 * members):
+                row = (field * 2 * members + c) * slots
+                part, member = c // members, c % members
+                if halved:
+                    at = (part * fields * members + field * members + member) * width
+                    keys = [(q, source) for q in range(group_lanes) for source in range(fields)]
+                else:
+                    at = c * width
+                    keys = [(q, field) for q in range(group_lanes)]
+                cut = slice(at, at + width)
+                even_in[h][row : row + slots, :] = jnp.concatenate([even[k][:, cut] for k in keys], axis=1)
+                odd_in[h][row : row + slots, :] = jnp.concatenate([odd[k][:, cut] for k in keys], axis=1)
+
+
+def scatter_orders(out_ref, fields, lat_groups, lat_rows, members, slots, halved, north, south):
     group_lanes = 128 // lat_rows
-    for field in range(fields):
+    width = lat_rows // fields if halved else lat_rows
+    for target in range(fields):
         for lat in range(lat_groups // 2):
             h, q = lat // group_lanes, lat % group_lanes
-            cut = slice(q * lat_rows, (q + 1) * lat_rows)
-            rows = [(field * per_field + c) * slots for c in range(per_field)]
+            at = q * lat_rows + (target * width if halved else 0)
+            cut = slice(at, at + width)
+            owners = range(fields) if halved else [target]
+            rows = [
+                (field * 2 * members + part * members + member) * slots
+                for part in range(2) for field in owners for member in range(members)
+            ]
             near = [north[h][row : row + slots, cut] for row in rows]
             far = [south[h][row : row + slots, cut] for row in rows]
-            out_ref[lat * fields + field] = jnp.concatenate(near, axis=1)
-            out_ref[(lat_groups - 1 - lat) * fields + field] = jnp.concatenate(far, axis=1)
-
-
-def sphere_body(degrees, devices, slots, lat_groups, lat_rows, members, with_mass, spec_ref, near_ref, far_in,
-                fixed_ref, out_ref, *rest):
+            out_ref[lat * fields + target] = jnp.concatenate(near, axis=1)
+            out_ref[(lat_groups - 1 - lat) * fields + target] = jnp.concatenate(far, axis=1)
+
+
+def sphere_body(degrees, devices, slots, lat_groups, lat_rows, members, with_mass, halves_in, halves_out, spec_ref, near_ref, far_in,
+                weight_ref, out_ref, *rest):
     far_ref, rest = (rest[0], rest[1:]) if with_mass else (far_in, rest)
     coef_ref, far_sem = rest[:2]
     halves = rest[2:]
@@ -515,7 +569,7 @@
     fields = devices // lat_groups
     per_field = 2 * members
     columns = fields * per_field
-    gather_orders(spec_ref, sign, fields, lat_groups, lat_rows, per_field, slots, even_in, odd_in)
+    gather_orders(spec_ref, sign, fields, lat_groups, lat_rows, members, slots, halves_in, even_in, odd_in)
     mass = None
 
     def pick(slot, parity):
@@ -523,7 +577,7 @@
         gain = 2.0 if slot else jnp.where(device == 0, 1.0, 2.0)
         pair = (even_in, odd_in)[parity]
         values = jnp.concatenate([pair[0][picked, :], pair[1][picked, :]], axis=1)
-        return values * (fixed_ref[slots + 2 : slots + 3, :] * gain)
+        return values * (weight_ref[...] * gain)
 
     def table(slot, parity):
         part_ref, offset, count = table_part(degrees, devices, slot, parity, near_ref, far_ref)
@@ -531,16 +585,15 @@
 
     if with_mass:
         mass = jnp.sum(pick(0, 0), axis=1, keepdims=True)
-    for slot in list(range(FAR_SLOTS, slots)) + list(range(FAR_SLOTS)):
-        if with_mass and slot == 0:
-            get_far.wait()
+
+    def analyse(slot):
         for parity in range(2):
             high, low, count = table(slot, parity)
             packed = pair_rows(pick(slot, parity))
             coef = dot_nt(packed, high) + dot_nt(packed, low)
             coef_ref[2 * slot + parity, :, 0:count] = pair_rows(coef[:columns] + coef[columns:])
 
-    for slot in range(slots):
+    def synthesise(slot):
         found = []
         for parity in range(2):
             high, low, count = table(slot, parity)
@@ -559,7 +612,20 @@
             north_out[h][picked, :] = north[:, 128 * h : 128 * h + 128]
             south_out[h][picked, :] = south[:, 128 * h : 128 * h + 128]
 
-    scatter_orders(out_ref, fields, lat_groups, lat_rows, per_field, slots, north_out, south_out)
+    near_slots, far_slots = range(FAR_SLOTS, slots), range(FAR_SLOTS)
+    early = FAR_SLOTS + (slots - FAR_SLOTS) // 2 if with_mass else FAR_SLOTS
+    for slot in near_slots:
+        analyse(slot)
+    for slot in range(FAR_SLOTS, early):
+        synthesise(slot)
+    if with_mass:
+        get_far.wait()
+    for slot in far_slots:
+        analyse(slot)
+    for slot in list(range(early, slots)) + list(far_slots):
+        synthesise(slot)
+
+    scatter_orders(out_ref, fields, lat_groups, lat_rows, members, slots, halves_out, north_out, south_out)
 
 
 def on_device_packed(precip):
@@ -621,9 +687,6 @@
         flat = spec.reshape(devices, slots, 2 * rows)
         return lax.all_to_all(flat, ("lat", "field"), split_axis=0, concat_axis=0, tiled=True)
 
-    def swap(value):
-        return lax.ppermute(value, "field", [(0, 1), (1, 0)])
-
     def bind(body, *bound):
         return lambda *refs: body(*bound, *refs)
 
@@ -633,11 +696,12 @@
     columns = fields * 2 * members
     signal = pltpu.SemaphoreType.DMA(())
 
-    def sphere(spec, near, far, with_mass):
+    def sphere(spec, near, far, with_mass, halves_in, halves_out):
         return call(
-            bind(sphere_body, degrees, devices, slots, lat_groups, lat_rows, members, with_mass),
+            bind(sphere_body, degrees, devices, slots, lat_groups, lat_rows, members, with_mass, halves_in,
+                 halves_out),
             (flat_shape, far_shape) if with_mass else flat_shape,
-            exchange(spec), near, far, fixed, far=(far,) if with_mass else (), name="sphere",
+            exchange(spec), near, far, weight, far=(far,) if with_mass else (), name="sphere",
             limit=8,
             scratch=[buffer((2 * slots, 2 * columns, 256), jnp.bfloat16), signal]
             + [buffer((columns * slots, 128))] * 8,
@@ -646,38 +710,38 @@
     def arrive(spec):
         return exchange(spec).reshape(spec_shape.shape)
 
-    near, far = call(
-        bind(legendre_body, degrees, devices, slots), (near_shape, far_shape), fixed, far=(fixed,), far_out=(1,),
+    weight_shape = jax.ShapeDtypeStruct((1, lat_total // 2), jnp.float32)
+    near, far, weight = call(
+        bind(legendre_body, degrees, devices, slots), (near_shape, far_shape, weight_shape), fixed, far=(fixed,), far_out=(1,),
         scratch=[buffer(fixed.shape)] + [buffer((slots, degrees))] * 2 + [buffer((degrees * slots, 128))] * 2
-        + [buffer(far_shape.shape, jnp.bfloat16), signal, signal],
+        + [buffer(far_shape.shape, jnp.bfloat16), signal, pltpu.SemaphoreType.DMA((FAR_SLOTS,))],
         cost=pl.CostEstimate(flops=40_000_000, bytes_accessed=16 << 20, transcendentals=0),
         name="legendre", limit=12,
     )
     field = precip.reshape(rows, lon_total)
+    seed = jnp.asarray(wave_seeds(lon_total, devices, slots))
     flipped, spec = call(
-        bind(first_body, lat_rows), (grid_shape, spec_shape), field, wave, far=(field, wave), far_out=(0, 1),
-        name="first", limit=8,
-        scratch=[buffer((rows, lon_total)), buffer(wave.shape, jnp.bfloat16), buffer((rows, lon_total)),
-                 buffer(spec_shape.shape), pltpu.SemaphoreType.DMA((2 + 2 * QUART,))],
+        bind(first_body, lat_rows, devices, slots), (grid_shape, spec_shape), field, seed, far=(field, seed),
+        far_out=(0, 1), name="first",
+        scratch=[buffer((rows, lon_total)), buffer(seed.shape), buffer(wave.shape, jnp.bfloat16),
+                 buffer((rows, lon_total)), buffer(spec_shape.shape), pltpu.SemaphoreType.DMA((3 + QUART,))],
     )
-    spec, far = sphere(spec, near, far, True)
-    clamped, total, scaled = call(
-        bind(mass_body, lat_rows), (grid_shape, sum_shape, grid_shape), arrive(spec), flipped, wave, name="mass",
+    spec, far = sphere(spec, near, far, True, False, True)
+    count = float(members * fields)
+    part_rows = lat_rows // fields
+    inverse_shape = jax.ShapeDtypeStruct((rows, 128), jnp.float32)
+    logs, inverse, spec = call(
+        bind(center_body, count, part_rows), (grid_shape, inverse_shape, spec_shape), arrive(spec), wave, name="center",
     )
-    count = float(members * fields)
-    logs, spec = call(
-        bind(center_body, count, lat_rows), (grid_shape, spec_shape), clamped, total, swap(total), wave,
-        name="center",
+    spec = sphere(spec, near, far, False, True, False)
+    spec = call(ratio_body, spec_shape, arrive(spec), flipped, inverse, wave, name="ratio")
+    spec = sphere(spec, near, far, False, False, True)
+    part_shape = jax.ShapeDtypeStruct(((members + 1) * part_rows, lon_total), jnp.float32)
+    keep, send = call(
+        bind(last_body, count, part_rows), (part_shape, part_shape), arrive(spec), logs, wave, name="last",
     )
-    spec = sphere(spec, near, far, False)
-    spec = call(ratio_body, spec_shape, arrive(spec), scaled, wave, name="ratio")
-    spec = sphere(spec, near, far, False)
-    clamped, total = call(
-        bind(last_body, lat_rows), (grid_shape, sum_shape), arrive(spec), logs, wave, name="last",
-    )
-    barycenter, logs = call(
-        bind(final_body, count, lat_rows), (sum_shape, grid_shape), clamped, total, swap(total), name="final",
-    )
+    got = lax.ppermute(send, "field", [(0, 1), (1, 0)])
+    barycenter, logs = call(bind(final_body, part_rows), (sum_shape, grid_shape), keep, got, name="final")
     return barycenter, logs.reshape(precip.shape)
 
 

time: 100 us -> 98.2 us (0.982)
    ppermute x2 -> x1, waiting for transfers between devices: 2.67 us -> 1.43 us  [on_device_packed(): got = lax.ppermute(send, 'field', [(0, 1), (1, 0)])]
    pallas_call x10 -> x9, Pallas kernels: 21.4 us -> 20.6 us  [call(): pl.pallas_call(body, out_shape=shapes[0] if single else shapes, in_specs=...]
  transfers between devices with their start and end apart: 3 -> 2, of which waited for: 3 -> 2; matrix products, arithmetic and copies ran while one was open for 0% -> 0% of each run, Pallas kernels for 7% -> 7%
where the time goes in v3:
time: 98.2 us; the launch traced here: 97.8 us
  blocking collectives  64.1 us (65%)
  Pallas kernels  20.6 us (21%)
  starting transfers between devices  7.37 us (8%)
  waiting for transfers between devices  5.02 us (5%)
    all_to_all x5, blocking collectives, exchange(): lax.all_to_all(flat, ('lat', 'field'), split_axis=0, concat_axis=0, tiled...  64.1 us
    pallas_call x9, Pallas kernels, call(): pl.pallas_call(body, out_shape=shapes[0] if single else shapes, in_specs=...  20.6 us
    all_to_all x1, starting transfers between devices, exchange(): lax.all_to_all(flat, ('lat', 'field'), split_axis=0, concat_axis=0, tiled...  7.3 us
    all_to_all x1, waiting for transfers between devices, exchange(): lax.all_to_all(flat, ('lat', 'field'), split_axis=0, concat_axis=0, tiled...  3.59 us
  transfers between devices with their start and end apart: 2, of which 2 were waited for; matrix products, arithmetic and copies ran while one was open for 0% of the time, Pallas kernels for 7%

profile of v3, /device:TPU:0, one launch (start us, length us, event | category | flops | bytes accessed | tf_op | source)
XLA Modules:
  0.0 97.8 jit_solution(16199682401939940327)
XLA Ops:
  0.6 2.4 %first.1 = (f32[64,1024]{1,0:T(8,128)}, f32[8,4,16,128]{3,2,1,0:T(8,128)}) custom-call(f32[64,1024]{1,0:T(8,128)} %bitcast.13, f32[96,256]{1,0:T(8,128)} %constant.8.clone.refs_1_), custom_call_target="tpu_custom_call" | custom-call | tf_op jit(solution)/shard_map/first/pallas_call | solution.py:675
  3.0 7.3 %all-to-all-start = ((f32[32,16,128]{2,1,0:T(8,128)}), f32[32,16,128]{2,1,0:T(8,128)S(1)}, u32[]{:S(2)}, u32[]{:S(2)}) async-start(f32[32,16,128]{2,1,0:T(8,128)} %bitcast.14), calls=%async_computation | async-start | bytes 524288 | tf_op jit(solution)/shard_map/all_to_all | solution.py:688
  10.3 7.0 %legendre.1 = (bf16[2,2912,256]{2,1,0:T(8,128)(2,1)S(1)}, bf16[2,1440,256]{2,1,0:T(8,128)(2,1)}, f32[1,256]{1,0:T(1,128)S(1)}) custom-call(f32[24,256]{1,0:T(8,128)} %constant.6.clone.refs_0_), custom_call_target="tpu_custom_call" | custom-call | flops 40000000 | bytes 16777216 | tf_op jit(solution)/shard_map/legendre/pallas_call | solution.py:675
  17.3 3.6 %all-to-all-done.refs_0_ = f32[32,16,128]{2,1,0:T(8,128)S(1)} async-done(((f32[32,16,128]{2,1,0:T(8,128)}), f32[32,16,128]{2,1,0:T(8,128)S(1)}, u32[]{:S(2)}, u32[]{:S(2)}) %all-to-all-start) | async-done | bytes 262176 | tf_op jit(solution)/shard_map/all_to_all | solution.py:688
  20.9 0.0 copy-start
  20.9 2.9 %sphere.3 = (f32[32,16,128]{2,1,0:T(8,128)S(1)}, bf16[2,1440,256]{2,1,0:T(8,128)(2,1)S(1)}) custom-call(f32[32,16,128]{2,1,0:T(8,128)S(1)} %all-to-all-done.refs_0_, bf16[2,2912,256]{2,1,0:T(8,128)(2,1)S(1)} %get-tuple-element.17.refs_1_, bf16[2,1440,256]{2,1,0:T(8,128)(2,1)} %get-tuple-element.18.refs_2_, f32[1,256]{1,0:T(1,128)S(1)} %get-tuple-element.19.refs_3_), custom_call_target="tpu_custom_call" | custom-call | tf_op jit(solution)/shard_map/sphere/pallas_call | solution.py:675
  23.8 12.8 %all_to_all.30 = f32[32,16,128]{2,1,0:T(8,128)S(1)} all-to-all(f32[32,16,128]{2,1,0:T(8,128)S(1)} %get-tuple-element.20), channel_id=1, replica_groups=mesh['lat'=16,'field'=2] {'lat','field'}, dimensions={0} | all-to-all | bytes 524288 | tf_op jit(solution)/shard_map/all_to_all | solution.py:688
  36.6 0.0 copy-done
  36.6 1.0 %center.1 = (f32[64,1024]{1,0:T(8,128)S(1)}, f32[64,128]{1,0:T(8,128)S(1)}, f32[8,4,16,128]{3,2,1,0:T(8,128)S(1)}) custom-call(f32[8,4,16,128]{3,2,1,0:T(8,128)S(1)} %bitcast.8, bf16[2,4,256,256]{3,2,1,0:T(8,128)(2,1)S(1)} %copy-done), custom_call_target="tpu_custom_call" | custom-call | tf_op jit(solution)/shard_map/center/pallas_call | solution.py:675
  37.7 12.8 %all_to_all.31.refs_0_ = f32[32,16,128]{2,1,0:T(8,128)S(1)} all-to-all(f32[32,16,128]{2,1,0:T(8,128)S(1)} %bitcast.12), channel_id=1, replica_groups=mesh['lat'=16,'field'=2] {'lat','field'}, dimensions={0} | all-to-all | bytes 524288 | tf_op jit(solution)/shard_map/all_to_all | solution.py:688
  50.5 0.0 copy-start.1
  50.5 2.5 %sphere.4 = f32[32,16,128]{2,1,0:T(8,128)S(1)} custom-call(f32[32,16,128]{2,1,0:T(8,128)S(1)} %all_to_all.31.refs_0_, bf16[2,2912,256]{2,1,0:T(8,128)(2,1)S(1)} %get-tuple-element.17.refs_1_, bf16[2,1440,256]{2,1,0:T(8,128)(2,1)S(1)} %get-tuple-element.22.refs_2_, f32[1,256]{1,0:T(1,128)S(1)} %get-tuple-element.19.refs_3_), custom_call_target="tpu_custom_call" | custom-call | tf_op jit(solution)/shard_map/sphere/pallas_call | solution.py:675
  52.9 12.8 %all_to_all.32 = f32[32,16,128]{2,1,0:T(8,128)S(1)} all-to-all(f32[32,16,128]{2,1,0:T(8,128)S(1)} %sphere.4), channel_id=1, replica_groups=mesh['lat'=16,'field'=2] {'lat','field'}, dimensions={0} | all-to-all | bytes 524288 | tf_op jit(solution)/shard_map/all_to_all | solution.py:688
  65.8 0.0 copy-done.1
  65.8 1.0 ratio.1
  66.7 12.8 %all_to_all.33.refs_0_ = f32[32,16,128]{2,1,0:T(8,128)S(1)} all-to-all(f32[32,16,128]{2,1,0:T(8,128)S(1)} %bitcast.10), channel_id=1, replica_groups=mesh['lat'=16,'field'=2] {'lat','field'}, dimensions={0} | all-to-all | bytes 524288 | tf_op jit(solution)/shard_map/all_to_all | solution.py:688
  79.6 2.6 %sphere.5 = f32[32,16,128]{2,1,0:T(8,128)S(1)} custom-call(f32[32,16,128]{2,1,0:T(8,128)S(1)} %all_to_all.33.refs_0_, bf16[2,2912,256]{2,1,0:T(8,128)(2,1)S(1)} %get-tuple-element.17.refs_1_, bf16[2,1440,256]{2,1,0:T(8,128)(2,1)S(1)} %get-tuple-element.22.refs_2_, f32[1,256]{1,0:T(1,128)S(1)} %get-tuple-element.19.refs_3_), custom_call_target="tpu_custom_call" | custom-call | tf_op jit(solution)/shard_map/sphere/pallas_call | solution.py:675
  82.2 12.8 %all_to_all.34 = f32[32,16,128]{2,1,0:T(8,128)S(1)} all-to-all(f32[32,16,128]{2,1,0:T(8,128)S(1)} %sphere.5), channel_id=1, replica_groups=mesh['lat'=16,'field'=2] {'lat','field'}, dimensions={0} | all-to-all | bytes 524288 | tf_op jit(solution)/shard_map/all_to_all | solution.py:688
  95.0 0.5 last.1
  95.5 0.1 collective-permute-start
  95.6 1.4 %collective-permute-done.refs_1_ = f32[48,1024]{1,0:T(8,128)S(1)} collective-permute-done((f32[48,1024]{1,0:T(8,128)S(1)}, f32[48,1024]{1,0:T(8,128)S(1)}, u32[]{:S(2)}, u32[]{:S(2)}) %collective-permute-start) | collective-permute-done | bytes 196640 | tf_op jit(solution)/shard_map/ppermute | solution.py:743
  97.0 0.8 final.1
Async XLA Ops:
  3.0 17.9 %all-to-all-start = ((f32[32,16,128]{2,1,0:T(8,128)}), f32[32,16,128]{2,1,0:T(8,128)S(1)}, u32[]{:S(2)}, u32[]{:S(2)}) async-start(f32[32,16,128]{2,1,0:T(8,128)} %bitcast.14), calls=%async_computation | async-start | bytes 524288 | tf_op jit(solution)/shard_map/all_to_all | solution.py:688
  20.9 15.7 %copy-start = (bf16[2,4,256,256]{3,2,1,0:T(8,128)(2,1)S(1)}, bf16[2,4,256,256]{3,2,1,0:T(8,128)(2,1)}, u32[]{:S(2)}) copy-start(bf16[2,4,256,256]{3,2,1,0:T(8,128)(2,1)} %constant.7.clone.refs_1_.wave_ref.refs_2_) | copy-start | bytes 3145732
  50.5 15.3 %copy-start.1 = (f32[64,1024]{1,0:T(8,128)S(1)}, f32[64,1024]{1,0:T(8,128)}, u32[]{:S(2)}) copy-start(f32[64,1024]{1,0:T(8,128)} %get-tuple-element.23.field_ref) | copy-start | bytes 786436
  95.5 1.5 %collective-permute-start = (f32[48,1024]{1,0:T(8,128)S(1)}, f32[48,1024]{1,0:T(8,128)S(1)}, u32[]{:S(2)}, u32[]{:S(2)}) collective-permute-start(f32[48,1024]{1,0:T(8,128)S(1)} %get-tuple-element.27), channel_id=1, source_target_pairs={{0,1},{1,0},{2,3},{3,2},{4,5},{5,4},{6,7},{7,6},{8,9},{9,8},{10,11... | collective-permute-start | bytes 589832 | tf_op jit(solution)/shard_map/ppermute | solution.py:743

commit v4 on v3

--- a/solution.py
+++ b/solution.py
@@ -509,50 +509,59 @@
         move_far(degrees, devices, slot, far_ref, far_hbm, far_sems).wait()
 
 
+def weave(first, second, width):
+    lanes = first.shape[-1]
+    even = lax.broadcasted_iota(jnp.int32, first.shape, first.ndim - 1) // width % 2 == 0
+    axis = first.ndim - 1
+    return (
+        jnp.where(even, first, pltpu.roll(second, width, axis)),
+        jnp.where(even, pltpu.roll(first, lanes - width, axis), second),
+    )
+
+
 def gather_orders(spec_ref, sign, fields, lat_groups, lat_rows, members, slots, halved, even_in, odd_in):
     group_lanes = 128 // lat_rows
-    width = lat_rows // fields if halved else lat_rows
     for h in range(2):
-        even, odd = {}, {}
+        even, odd = [], []
         for q in range(group_lanes):
+            lat = h * group_lanes + q
+            pair = ([], [])
             for source in range(fields):
-                lat = h * group_lanes + q
                 north = spec_ref[lat * fields + source]
                 south = spec_ref[(lat_groups - 1 - lat) * fields + source] * sign
-                even[q, source] = north + south
-                odd[q, source] = north - south
+                pair[0].append(north + south)
+                pair[1].append(north - south)
+            if halved:
+                pair = [weave(*p, lat_rows // 2) for p in pair]
+            even.append(pair[0])
+            odd.append(pair[1])
         for field in range(fields):
             for c in range(2 * members):
                 row = (field * 2 * members + c) * slots
                 part, member = c // members, c % members
-                if halved:
-                    at = (part * fields * members + field * members + member) * width
-                    keys = [(q, source) for q in range(group_lanes) for source in range(fields)]
-                else:
-                    at = c * width
-                    keys = [(q, field) for q in range(group_lanes)]
-                cut = slice(at, at + width)
-                even_in[h][row : row + slots, :] = jnp.concatenate([even[k][:, cut] for k in keys], axis=1)
-                odd_in[h][row : row + slots, :] = jnp.concatenate([odd[k][:, cut] for k in keys], axis=1)
+                block, at = (member, part * fields + field) if halved else (field, c)
+                cut = slice(at * lat_rows, (at + 1) * lat_rows)
+                even_in[h][row : row + slots, :] = jnp.concatenate([e[block][:, cut] for e in even], axis=1)
+                odd_in[h][row : row + slots, :] = jnp.concatenate([o[block][:, cut] for o in odd], axis=1)
 
 
 def scatter_orders(out_ref, fields, lat_groups, lat_rows, members, slots, halved, north, south):
     group_lanes = 128 // lat_rows
-    width = lat_rows // fields if halved else lat_rows
-    for target in range(fields):
-        for lat in range(lat_groups // 2):
-            h, q = lat // group_lanes, lat % group_lanes
-            at = q * lat_rows + (target * width if halved else 0)
-            cut = slice(at, at + width)
-            owners = range(fields) if halved else [target]
-            rows = [
-                (field * 2 * members + part * members + member) * slots
-                for part in range(2) for field in owners for member in range(members)
-            ]
-            near = [north[h][row : row + slots, cut] for row in rows]
-            far = [south[h][row : row + slots, cut] for row in rows]
-            out_ref[lat * fields + target] = jnp.concatenate(near, axis=1)
-            out_ref[(lat_groups - 1 - lat) * fields + target] = jnp.concatenate(far, axis=1)
+    for lat in range(lat_groups // 2):
+        h, q = lat // group_lanes, lat % group_lanes
+        cut = slice(q * lat_rows, (q + 1) * lat_rows)
+        for source, place in ((north, lat), (south, lat_groups - 1 - lat)):
+            blocks = []
+            for block in range(2):
+                if halved:
+                    owners = [(field, part, block) for part in range(2) for field in range(fields)]
+                else:
+                    owners = [(block, part, member) for part in range(2) for member in range(members)]
+                rows = [((field * 2 + part) * members + member) * slots for field, part, member in owners]
+                blocks.append(jnp.concatenate([source[h][row : row + slots, cut] for row in rows], axis=1))
+            if halved:
+                blocks = weave(*blocks, lat_rows // 2)
+            out_ref[place * fields], out_ref[place * fields + 1] = blocks
 
 
 def sphere_body(degrees, devices, slots, lat_groups, lat_rows, members, with_mass, halves_in, halves_out, spec_ref, near_ref, far_in,
@@ -613,7 +622,7 @@
             south_out[h][picked, :] = south[:, 128 * h : 128 * h + 128]
 
     near_slots, far_slots = range(FAR_SLOTS, slots), range(FAR_SLOTS)
-    early = FAR_SLOTS + (slots - FAR_SLOTS) // 2 if with_mass else FAR_SLOTS
+    early = slots if with_mass else FAR_SLOTS
     for slot in near_slots:
         analyse(slot)
     for slot in range(FAR_SLOTS, early):
@@ -756,7 +765,7 @@
         and lon_total == 4 * lat_total // 2
         and lat_total == 512
         and 2 * members * lat_rows == 128
-        and fields * 2 * members == 8
+        and members == 2
         and lat_groups % 2 == 0
         and devices % QUART == 0
         and degrees % (8 * devices) == 0

time: 98.2 us -> 97.5 us (level)
  no operation moved by 1% of the time
where the time goes in v4:
time: 97.5 us; the launch traced here: 97.1 us
  blocking collectives  64.1 us (66%)
  Pallas kernels  20 us (21%)
  starting transfers between devices  7.37 us (8%)
  waiting for transfers between devices  5.02 us (5%)
    all_to_all x5, blocking collectives, exchange(): lax.all_to_all(flat, ('lat', 'field'), split_axis=0, concat_axis=0, tiled...  64.1 us
    pallas_call x9, Pallas kernels, call(): pl.pallas_call(body, out_shape=shapes[0] if single else shapes, in_specs=...  20 us
    all_to_all x1, starting transfers between devices, exchange(): lax.all_to_all(flat, ('lat', 'field'), split_axis=0, concat_axis=0, tiled...  7.3 us
    all_to_all x1, waiting for transfers between devices, exchange(): lax.all_to_all(flat, ('lat', 'field'), split_axis=0, concat_axis=0, tiled...  3.59 us
  transfers between devices with their start and end apart: 2, of which 2 were waited for; matrix products, arithmetic and copies ran while one was open for 0% of the time, Pallas kernels for 7%

profile of v4, /device:TPU:0, one launch (start us, length us, event | category | flops | bytes accessed | tf_op | source)
XLA Modules:
  0.0 97.1 jit_solution(13755696425034438506)
XLA Ops:
  0.6 2.4 %first.1 = (f32[64,1024]{1,0:T(8,128)}, f32[8,4,16,128]{3,2,1,0:T(8,128)}) custom-call(f32[64,1024]{1,0:T(8,128)} %bitcast.13, f32[96,256]{1,0:T(8,128)} %constant.8.clone.refs_1_), custom_call_target="tpu_custom_call" | custom-call | tf_op jit(solution)/shard_map/first/pallas_call | solution.py:684
  3.0 7.3 %all-to-all-start = ((f32[32,16,128]{2,1,0:T(8,128)}), f32[32,16,128]{2,1,0:T(8,128)S(1)}, u32[]{:S(2)}, u32[]{:S(2)}) async-start(f32[32,16,128]{2,1,0:T(8,128)} %bitcast.14), calls=%async_computation | async-start | bytes 524288 | tf_op jit(solution)/shard_map/all_to_all | solution.py:697
  10.3 7.0 %legendre.1 = (bf16[2,2912,256]{2,1,0:T(8,128)(2,1)S(1)}, bf16[2,1440,256]{2,1,0:T(8,128)(2,1)}, f32[1,256]{1,0:T(1,128)S(1)}) custom-call(f32[24,256]{1,0:T(8,128)} %constant.6.clone.refs_0_), custom_call_target="tpu_custom_call" | custom-call | flops 40000000 | bytes 16777216 | tf_op jit(solution)/shard_map/legendre/pallas_call | solution.py:684
  17.3 3.6 %all-to-all-done.refs_0_ = f32[32,16,128]{2,1,0:T(8,128)S(1)} async-done(((f32[32,16,128]{2,1,0:T(8,128)}), f32[32,16,128]{2,1,0:T(8,128)S(1)}, u32[]{:S(2)}, u32[]{:S(2)}) %all-to-all-start) | async-done | bytes 262176 | tf_op jit(solution)/shard_map/all_to_all | solution.py:697
  20.9 0.0 copy-start
  20.9 2.5 %sphere.3 = (f32[32,16,128]{2,1,0:T(8,128)S(1)}, bf16[2,1440,256]{2,1,0:T(8,128)(2,1)S(1)}) custom-call(f32[32,16,128]{2,1,0:T(8,128)S(1)} %all-to-all-done.refs_0_, bf16[2,2912,256]{2,1,0:T(8,128)(2,1)S(1)} %get-tuple-element.17.refs_1_, bf16[2,1440,256]{2,1,0:T(8,128)(2,1)} %get-tuple-element.18.refs_2_, f32[1,256]{1,0:T(1,128)S(1)} %get-tuple-element.19.refs_3_), custom_call_target="tpu_custom_call" | custom-call | tf_op jit(solution)/shard_map/sphere/pallas_call | solution.py:684
  23.4 12.8 %all_to_all.30 = f32[32,16,128]{2,1,0:T(8,128)S(1)} all-to-all(f32[32,16,128]{2,1,0:T(8,128)S(1)} %get-tuple-element.20), channel_id=1, replica_groups=mesh['lat'=16,'field'=2] {'lat','field'}, dimensions={0} | all-to-all | bytes 524288 | tf_op jit(solution)/shard_map/all_to_all | solution.py:697
  36.2 0.0 copy-done
  36.2 1.0 %center.1 = (f32[64,1024]{1,0:T(8,128)S(1)}, f32[64,128]{1,0:T(8,128)S(1)}, f32[8,4,16,128]{3,2,1,0:T(8,128)S(1)}) custom-call(f32[8,4,16,128]{3,2,1,0:T(8,128)S(1)} %bitcast.8, bf16[2,4,256,256]{3,2,1,0:T(8,128)(2,1)S(1)} %copy-done), custom_call_target="tpu_custom_call" | custom-call | tf_op jit(solution)/shard_map/center/pallas_call | solution.py:684
  37.3 12.8 %all_to_all.31.refs_0_ = f32[32,16,128]{2,1,0:T(8,128)S(1)} all-to-all(f32[32,16,128]{2,1,0:T(8,128)S(1)} %bitcast.12), channel_id=1, replica_groups=mesh['lat'=16,'field'=2] {'lat','field'}, dimensions={0} | all-to-all | bytes 524288 | tf_op jit(solution)/shard_map/all_to_all | solution.py:697
  50.1 0.0 copy-start.1
  50.1 2.4 %sphere.4 = f32[32,16,128]{2,1,0:T(8,128)S(1)} custom-call(f32[32,16,128]{2,1,0:T(8,128)S(1)} %all_to_all.31.refs_0_, bf16[2,2912,256]{2,1,0:T(8,128)(2,1)S(1)} %get-tuple-element.17.refs_1_, bf16[2,1440,256]{2,1,0:T(8,128)(2,1)S(1)} %get-tuple-element.22.refs_2_, f32[1,256]{1,0:T(1,128)S(1)} %get-tuple-element.19.refs_3_), custom_call_target="tpu_custom_call" | custom-call | tf_op jit(solution)/shard_map/sphere/pallas_call | solution.py:684
  52.5 12.8 %all_to_all.32 = f32[32,16,128]{2,1,0:T(8,128)S(1)} all-to-all(f32[32,16,128]{2,1,0:T(8,128)S(1)} %sphere.4), channel_id=1, replica_groups=mesh['lat'=16,'field'=2] {'lat','field'}, dimensions={0} | all-to-all | bytes 524288 | tf_op jit(solution)/shard_map/all_to_all | solution.py:697
  65.3 0.0 copy-done.1
  65.3 1.0 %ratio.1 = f32[8,4,16,128]{3,2,1,0:T(8,128)S(1)} custom-call(f32[8,4,16,128]{3,2,1,0:T(8,128)S(1)} %bitcast.9, f32[64,1024]{1,0:T(8,128)S(1)} %copy-done.1, f32[64,128]{1,0:T(8,128)S(1)} %get-tuple-element.24.inverse_ref, bf16[2,4,256,256]{3,2,1,0:T(8,128)(2,1)S(1)} %copy-done), custom_call_target="tpu_custom_call" | custom-call | tf_op jit(solution)/shard_map/ratio/pallas_call | solution.py:684
  66.3 12.8 %all_to_all.33.refs_0_ = f32[32,16,128]{2,1,0:T(8,128)S(1)} all-to-all(f32[32,16,128]{2,1,0:T(8,128)S(1)} %bitcast.10), channel_id=1, replica_groups=mesh['lat'=16,'field'=2] {'lat','field'}, dimensions={0} | all-to-all | bytes 524288 | tf_op jit(solution)/shard_map/all_to_all | solution.py:697
  79.1 2.4 %sphere.5 = f32[32,16,128]{2,1,0:T(8,128)S(1)} custom-call(f32[32,16,128]{2,1,0:T(8,128)S(1)} %all_to_all.33.refs_0_, bf16[2,2912,256]{2,1,0:T(8,128)(2,1)S(1)} %get-tuple-element.17.refs_1_, bf16[2,1440,256]{2,1,0:T(8,128)(2,1)S(1)} %get-tuple-element.22.refs_2_, f32[1,256]{1,0:T(1,128)S(1)} %get-tuple-element.19.refs_3_), custom_call_target="tpu_custom_call" | custom-call | tf_op jit(solution)/shard_map/sphere/pallas_call | solution.py:684
  81.5 12.8 %all_to_all.34 = f32[32,16,128]{2,1,0:T(8,128)S(1)} all-to-all(f32[32,16,128]{2,1,0:T(8,128)S(1)} %sphere.5), channel_id=1, replica_groups=mesh['lat'=16,'field'=2] {'lat','field'}, dimensions={0} | all-to-all | bytes 524288 | tf_op jit(solution)/shard_map/all_to_all | solution.py:697
  94.3 0.5 last.1
  94.8 0.1 collective-permute-start
  94.9 1.4 %collective-permute-done.refs_1_ = f32[48,1024]{1,0:T(8,128)S(1)} collective-permute-done((f32[48,1024]{1,0:T(8,128)S(1)}, f32[48,1024]{1,0:T(8,128)S(1)}, u32[]{:S(2)}, u32[]{:S(2)}) %collective-permute-start) | collective-permute-done | bytes 196640 | tf_op jit(solution)/shard_map/ppermute | solution.py:752
  96.3 0.8 final.1
Async XLA Ops:
  3.0 17.9 %all-to-all-start = ((f32[32,16,128]{2,1,0:T(8,128)}), f32[32,16,128]{2,1,0:T(8,128)S(1)}, u32[]{:S(2)}, u32[]{:S(2)}) async-start(f32[32,16,128]{2,1,0:T(8,128)} %bitcast.14), calls=%async_computation | async-start | bytes 524288 | tf_op jit(solution)/shard_map/all_to_all | solution.py:697
  20.9 15.3 %copy-start = (bf16[2,4,256,256]{3,2,1,0:T(8,128)(2,1)S(1)}, bf16[2,4,256,256]{3,2,1,0:T(8,128)(2,1)}, u32[]{:S(2)}) copy-start(bf16[2,4,256,256]{3,2,1,0:T(8,128)(2,1)} %constant.7.clone.refs_1_.wave_ref.refs_2_) | copy-start | bytes 3145732
  50.1 15.2 %copy-start.1 = (f32[64,1024]{1,0:T(8,128)S(1)}, f32[64,1024]{1,0:T(8,128)}, u32[]{:S(2)}) copy-start(f32[64,1024]{1,0:T(8,128)} %get-tuple-element.23.field_ref) | copy-start | bytes 786436
  94.8 1.5 %collective-permute-start = (f32[48,1024]{1,0:T(8,128)S(1)}, f32[48,1024]{1,0:T(8,128)S(1)}, u32[]{:S(2)}, u32[]{:S(2)}) collective-permute-start(f32[48,1024]{1,0:T(8,128)S(1)} %get-tuple-element.27), channel_id=1, source_target_pairs={{0,1},{1,0},{2,3},{3,2},{4,5},{5,4},{6,7},{7,6},{8,9},{9,8},{10,11... | collective-permute-start | bytes 589832 | tf_op jit(solution)/shard_map/ppermute | solution.py:752

commit v5 on v4

--- a/solution.py
+++ b/solution.py
@@ -337,7 +337,7 @@
     get_seed.wait()
     grow_waves(seed_ref, wave_ref, devices, slots)
     get_field.wait()
-    flipped_ref[...] = flip_rows(field_ref[...], in_south(), lat_rows)
+    flipped_ref[...] = flip_rows(field_ref[...], in_south(), lat_rows) * 2.0**-8
     put_flipped.start()
     forward_waves(flipped_ref[...], wave_ref, out_ref, put_wave)
     put_flipped.wait()
@@ -713,7 +713,7 @@
             exchange(spec), near, far, weight, far=(far,) if with_mass else (), name="sphere",
             limit=8,
             scratch=[buffer((2 * slots, 2 * columns, 256), jnp.bfloat16), signal]
-            + [buffer((columns * slots, 128))] * 8,
+            + [buffer((columns * slots + slots, 128))] * 8,
         )
 
     def arrive(spec):
@@ -722,7 +722,7 @@
     weight_shape = jax.ShapeDtypeStruct((1, lat_total // 2), jnp.float32)
     near, far, weight = call(
         bind(legendre_body, degrees, devices, slots), (near_shape, far_shape, weight_shape), fixed, far=(fixed,), far_out=(1,),
-        scratch=[buffer(fixed.shape)] + [buffer((slots, degrees))] * 2 + [buffer((degrees * slots, 128))] * 2
+        scratch=[buffer(fixed.shape)] + [buffer((slots, degrees))] * 2 + [buffer((degrees * slots + 2 * slots, 128))] * 2
         + [buffer(far_shape.shape, jnp.bfloat16), signal, pltpu.SemaphoreType.DMA((FAR_SLOTS,))],
         cost=pl.CostEstimate(flops=40_000_000, bytes_accessed=16 << 20, transcendentals=0),
         name="legendre", limit=12,

time: 97.5 us -> 97.5 us (level)
  no operation moved by 1% of the time
where the time goes in v5:
time: 97.5 us; the launch traced here: 97.1 us
  blocking collectives  64.1 us (66%)
  Pallas kernels  20 us (21%)
  starting transfers between devices  7.37 us (8%)
  waiting for transfers between devices  5.03 us (5%)
    all_to_all x5, blocking collectives, exchange(): lax.all_to_all(flat, ('lat', 'field'), split_axis=0, concat_axis=0, tiled...  64.1 us
    pallas_call x9, Pallas kernels, call(): pl.pallas_call(body, out_shape=shapes[0] if single else shapes, in_specs=...  20 us
    all_to_all x1, starting transfers between devices, exchange(): lax.all_to_all(flat, ('lat', 'field'), split_axis=0, concat_axis=0, tiled...  7.3 us
    all_to_all x1, waiting for transfers between devices, exchange(): lax.all_to_all(flat, ('lat', 'field'), split_axis=0, concat_axis=0, tiled...  3.6 us
  transfers between devices with their start and end apart: 2, of which 2 were waited for; matrix products, arithmetic and copies ran while one was open for 0% of the time, Pallas kernels for 7%

profile of v5, /device:TPU:0, one launch (start us, length us, event | category | flops | bytes accessed | tf_op | source)
XLA Modules:
  0.0 97.1 jit_solution(7126353440816896115)
XLA Ops:
  0.6 2.4 %first.1 = (f32[64,1024]{1,0:T(8,128)}, f32[8,4,16,128]{3,2,1,0:T(8,128)}) custom-call(f32[64,1024]{1,0:T(8,128)} %bitcast.13, f32[96,256]{1,0:T(8,128)} %constant.8.clone.refs_1_), custom_call_target="tpu_custom_call" | custom-call | tf_op jit(solution)/shard_map/first/pallas_call | solution.py:684
  3.0 7.3 %all-to-all-start = ((f32[32,16,128]{2,1,0:T(8,128)}), f32[32,16,128]{2,1,0:T(8,128)S(1)}, u32[]{:S(2)}, u32[]{:S(2)}) async-start(f32[32,16,128]{2,1,0:T(8,128)} %bitcast.14), calls=%async_computation | async-start | bytes 524288 | tf_op jit(solution)/shard_map/all_to_all | solution.py:697
  10.3 7.0 %legendre.1 = (bf16[2,2912,256]{2,1,0:T(8,128)(2,1)S(1)}, bf16[2,1440,256]{2,1,0:T(8,128)(2,1)}, f32[1,256]{1,0:T(1,128)S(1)}) custom-call(f32[24,256]{1,0:T(8,128)} %constant.6.clone.refs_0_), custom_call_target="tpu_custom_call" | custom-call | flops 40000000 | bytes 16777216 | tf_op jit(solution)/shard_map/legendre/pallas_call | solution.py:684
  17.3 3.6 %all-to-all-done.refs_0_ = f32[32,16,128]{2,1,0:T(8,128)S(1)} async-done(((f32[32,16,128]{2,1,0:T(8,128)}), f32[32,16,128]{2,1,0:T(8,128)S(1)}, u32[]{:S(2)}, u32[]{:S(2)}) %all-to-all-start) | async-done | bytes 262176 | tf_op jit(solution)/shard_map/all_to_all | solution.py:697
  20.9 0.0 copy-start
  20.9 2.5 %sphere.3 = (f32[32,16,128]{2,1,0:T(8,128)S(1)}, bf16[2,1440,256]{2,1,0:T(8,128)(2,1)S(1)}) custom-call(f32[32,16,128]{2,1,0:T(8,128)S(1)} %all-to-all-done.refs_0_, bf16[2,2912,256]{2,1,0:T(8,128)(2,1)S(1)} %get-tuple-element.17.refs_1_, bf16[2,1440,256]{2,1,0:T(8,128)(2,1)} %get-tuple-element.18.refs_2_, f32[1,256]{1,0:T(1,128)S(1)} %get-tuple-element.19.refs_3_), custom_call_target="tpu_custom_call" | custom-call | tf_op jit(solution)/shard_map/sphere/pallas_call | solution.py:684
  23.4 12.8 %all_to_all.30 = f32[32,16,128]{2,1,0:T(8,128)S(1)} all-to-all(f32[32,16,128]{2,1,0:T(8,128)S(1)} %get-tuple-element.20), channel_id=1, replica_groups=mesh['lat'=16,'field'=2] {'lat','field'}, dimensions={0} | all-to-all | bytes 524288 | tf_op jit(solution)/shard_map/all_to_all | solution.py:697
  36.2 0.0 copy-done
  36.3 1.0 %center.1 = (f32[64,1024]{1,0:T(8,128)S(1)}, f32[64,128]{1,0:T(8,128)S(1)}, f32[8,4,16,128]{3,2,1,0:T(8,128)S(1)}) custom-call(f32[8,4,16,128]{3,2,1,0:T(8,128)S(1)} %bitcast.8, bf16[2,4,256,256]{3,2,1,0:T(8,128)(2,1)S(1)} %copy-done), custom_call_target="tpu_custom_call" | custom-call | tf_op jit(solution)/shard_map/center/pallas_call | solution.py:684
  37.3 12.8 %all_to_all.31.refs_0_ = f32[32,16,128]{2,1,0:T(8,128)S(1)} all-to-all(f32[32,16,128]{2,1,0:T(8,128)S(1)} %bitcast.12), channel_id=1, replica_groups=mesh['lat'=16,'field'=2] {'lat','field'}, dimensions={0} | all-to-all | bytes 524288 | tf_op jit(solution)/shard_map/all_to_all | solution.py:697
  50.1 0.0 copy-start.1
  50.1 2.4 %sphere.4 = f32[32,16,128]{2,1,0:T(8,128)S(1)} custom-call(f32[32,16,128]{2,1,0:T(8,128)S(1)} %all_to_all.31.refs_0_, bf16[2,2912,256]{2,1,0:T(8,128)(2,1)S(1)} %get-tuple-element.17.refs_1_, bf16[2,1440,256]{2,1,0:T(8,128)(2,1)S(1)} %get-tuple-element.22.refs_2_, f32[1,256]{1,0:T(1,128)S(1)} %get-tuple-element.19.refs_3_), custom_call_target="tpu_custom_call" | custom-call | tf_op jit(solution)/shard_map/sphere/pallas_call | solution.py:684
  52.5 12.8 %all_to_all.32 = f32[32,16,128]{2,1,0:T(8,128)S(1)} all-to-all(f32[32,16,128]{2,1,0:T(8,128)S(1)} %sphere.4), channel_id=1, replica_groups=mesh['lat'=16,'field'=2] {'lat','field'}, dimensions={0} | all-to-all | bytes 524288 | tf_op jit(solution)/shard_map/all_to_all | solution.py:697
  65.3 0.0 copy-done.1
  65.3 1.0 %ratio.1 = f32[8,4,16,128]{3,2,1,0:T(8,128)S(1)} custom-call(f32[8,4,16,128]{3,2,1,0:T(8,128)S(1)} %bitcast.9, f32[64,1024]{1,0:T(8,128)S(1)} %copy-done.1, f32[64,128]{1,0:T(8,128)S(1)} %get-tuple-element.24.inverse_ref, bf16[2,4,256,256]{3,2,1,0:T(8,128)(2,1)S(1)} %copy-done), custom_call_target="tpu_custom_call" | custom-call | tf_op jit(solution)/shard_map/ratio/pallas_call | solution.py:684
  66.3 12.8 %all_to_all.33.refs_0_ = f32[32,16,128]{2,1,0:T(8,128)S(1)} all-to-all(f32[32,16,128]{2,1,0:T(8,128)S(1)} %bitcast.10), channel_id=1, replica_groups=mesh['lat'=16,'field'=2] {'lat','field'}, dimensions={0} | all-to-all | bytes 524288 | tf_op jit(solution)/shard_map/all_to_all | solution.py:697
  79.1 2.4 %sphere.5 = f32[32,16,128]{2,1,0:T(8,128)S(1)} custom-call(f32[32,16,128]{2,1,0:T(8,128)S(1)} %all_to_all.33.refs_0_, bf16[2,2912,256]{2,1,0:T(8,128)(2,1)S(1)} %get-tuple-element.17.refs_1_, bf16[2,1440,256]{2,1,0:T(8,128)(2,1)S(1)} %get-tuple-element.22.refs_2_, f32[1,256]{1,0:T(1,128)S(1)} %get-tuple-element.19.refs_3_), custom_call_target="tpu_custom_call" | custom-call | tf_op jit(solution)/shard_map/sphere/pallas_call | solution.py:684
  81.5 12.8 %all_to_all.34 = f32[32,16,128]{2,1,0:T(8,128)S(1)} all-to-all(f32[32,16,128]{2,1,0:T(8,128)S(1)} %sphere.5), channel_id=1, replica_groups=mesh['lat'=16,'field'=2] {'lat','field'}, dimensions={0} | all-to-all | bytes 524288 | tf_op jit(solution)/shard_map/all_to_all | solution.py:697
  94.3 0.5 last.1
  94.8 0.1 collective-permute-start
  94.9 1.4 %collective-permute-done.refs_1_ = f32[48,1024]{1,0:T(8,128)S(1)} collective-permute-done((f32[48,1024]{1,0:T(8,128)S(1)}, f32[48,1024]{1,0:T(8,128)S(1)}, u32[]{:S(2)}, u32[]{:S(2)}) %collective-permute-start) | collective-permute-done | bytes 196640 | tf_op jit(solution)/shard_map/ppermute | solution.py:752
  96.4 0.8 final.1
Async XLA Ops:
  3.0 17.9 %all-to-all-start = ((f32[32,16,128]{2,1,0:T(8,128)}), f32[32,16,128]{2,1,0:T(8,128)S(1)}, u32[]{:S(2)}, u32[]{:S(2)}) async-start(f32[32,16,128]{2,1,0:T(8,128)} %bitcast.14), calls=%async_computation | async-start | bytes 524288 | tf_op jit(solution)/shard_map/all_to_all | solution.py:697
  20.9 15.3 %copy-start = (bf16[2,4,256,256]{3,2,1,0:T(8,128)(2,1)S(1)}, bf16[2,4,256,256]{3,2,1,0:T(8,128)(2,1)}, u32[]{:S(2)}) copy-start(bf16[2,4,256,256]{3,2,1,0:T(8,128)(2,1)} %constant.7.clone.refs_1_.wave_ref.refs_2_) | copy-start | bytes 3145732
  50.1 15.2 %copy-start.1 = (f32[64,1024]{1,0:T(8,128)S(1)}, f32[64,1024]{1,0:T(8,128)}, u32[]{:S(2)}) copy-start(f32[64,1024]{1,0:T(8,128)} %get-tuple-element.23.field_ref) | copy-start | bytes 786436
  94.8 1.5 %collective-permute-start = (f32[48,1024]{1,0:T(8,128)S(1)}, f32[48,1024]{1,0:T(8,128)S(1)}, u32[]{:S(2)}, u32[]{:S(2)}) collective-permute-start(f32[48,1024]{1,0:T(8,128)S(1)} %get-tuple-element.27), channel_id=1, source_target_pairs={{0,1},{1,0},{2,3},{3,2},{4,5},{5,4},{6,7},{7,6},{8,9},{9,8},{10,11... | collective-permute-start | bytes 589832 | tf_op jit(solution)/shard_map/ppermute | solution.py:752

commit v6 on v5

--- a/solution.py
+++ b/solution.py
@@ -324,23 +324,22 @@
     return lax.axis_index("lat") >= lax.axis_size("lat") // 2
 
 
-def first_body(lat_rows, devices, slots, field_hbm, seed_hbm, flipped_hbm, out_hbm, field_ref, seed_ref, wave_ref,
-               flipped_ref, out_ref, sems):
+def oriented(field, lat_rows):
+    return flip_rows(field, in_south(), lat_rows) * 2.0**-8
+
+
+def first_body(lat_rows, devices, slots, field_hbm, seed_hbm, out_hbm, field_ref, seed_ref, wave_ref, out_ref, sems):
     get_field = pltpu.make_async_copy(field_hbm, field_ref, sems.at[0])
     get_seed = pltpu.make_async_copy(seed_hbm, seed_ref, sems.at[1])
-    put_flipped = pltpu.make_async_copy(flipped_ref, flipped_hbm, sems.at[2])
     put_wave = [
-        pltpu.make_async_copy(out_ref.at[:, r], out_hbm.at[:, r], sems.at[3 + r]) for r in range(QUART)
+        pltpu.make_async_copy(out_ref.at[:, r], out_hbm.at[:, r], sems.at[2 + r]) for r in range(QUART)
     ]
     get_seed.start()
     get_field.start()
     get_seed.wait()
     grow_waves(seed_ref, wave_ref, devices, slots)
     get_field.wait()
-    flipped_ref[...] = flip_rows(field_ref[...], in_south(), lat_rows) * 2.0**-8
-    put_flipped.start()
-    forward_waves(flipped_ref[...], wave_ref, out_ref, put_wave)
-    put_flipped.wait()
+    forward_waves(oriented(field_ref[...], lat_rows), wave_ref, out_ref, put_wave)
     for copy in put_wave:
         copy.wait()
 
@@ -370,9 +369,9 @@
     inverse_ref[...] = jnp.broadcast_to(jnp.concatenate([p for p in parts for _ in range(2)], axis=0), inverse_ref.shape)
 
 
-def ratio_body(spec_ref, field_ref, inverse_ref, wave_ref, out_ref):
+def ratio_body(lat_rows, spec_ref, field_ref, inverse_ref, wave_ref, out_ref):
     blurred, _ = inverse_waves(spec_ref, wave_ref)
-    scaled = field_ref[...] * inverse_ref[:, 0:1]
+    scaled = oriented(field_ref[...], lat_rows) * inverse_ref[:, 0:1]
     forward_waves(scaled / jnp.maximum(blurred, floor_value), wave_ref, out_ref)
 
 
@@ -547,21 +546,25 @@
 
 def scatter_orders(out_ref, fields, lat_groups, lat_rows, members, slots, halved, north, south):
     group_lanes = 128 // lat_rows
-    for lat in range(lat_groups // 2):
-        h, q = lat // group_lanes, lat % group_lanes
-        cut = slice(q * lat_rows, (q + 1) * lat_rows)
-        for source, place in ((north, lat), (south, lat_groups - 1 - lat)):
-            blocks = []
-            for block in range(2):
+    columns = fields * 2 * members
+    for h in range(2):
+        for source, mirrored in ((north, False), (south, True)):
+            values = [source[h][pl.ds(column, slots, stride=columns), :] for column in range(columns)]
+            for q in range(group_lanes):
+                lat = h * group_lanes + q
+                place = lat_groups - 1 - lat if mirrored else lat
+                cut = slice(q * lat_rows, (q + 1) * lat_rows)
+                blocks = []
+                for block in range(2):
+                    if halved:
+                        owners = [(field, part, block) for part in range(2) for field in range(fields)]
+                    else:
+                        owners = [(block, part, member) for part in range(2) for member in range(members)]
+                    picked = [(field * 2 + part) * members + member for field, part, member in owners]
+                    blocks.append(jnp.concatenate([values[column][:, cut] for column in picked], axis=1))
                 if halved:
-                    owners = [(field, part, block) for part in range(2) for field in range(fields)]
-                else:
-                    owners = [(block, part, member) for part in range(2) for member in range(members)]
-                rows = [((field * 2 + part) * members + member) * slots for field, part, member in owners]
-                blocks.append(jnp.concatenate([source[h][row : row + slots, cut] for row in rows], axis=1))
-            if halved:
-                blocks = weave(*blocks, lat_rows // 2)
-            out_ref[place * fields], out_ref[place * fields + 1] = blocks
+                    blocks = weave(*blocks, lat_rows // 2)
+                out_ref[place * fields], out_ref[place * fields + 1] = blocks
 
 
 def sphere_body(degrees, devices, slots, lat_groups, lat_rows, members, with_mass, halves_in, halves_out, spec_ref, near_ref, far_in,
@@ -616,7 +619,7 @@
             which = lax.broadcasted_iota(jnp.int32, north.shape, 0) % per_field
             spare = (which >= members) & (device == 0)
             north, south = jnp.where(spare, spread, north), jnp.where(spare, spread, south)
-        picked = pl.ds(slot, columns, stride=slots)
+        picked = slice(slot * columns, (slot + 1) * columns)
         for h in range(2):
             north_out[h][picked, :] = north[:, 128 * h : 128 * h + 128]
             south_out[h][picked, :] = south[:, 128 * h : 128 * h + 128]
@@ -729,11 +732,11 @@
     )
     field = precip.reshape(rows, lon_total)
     seed = jnp.asarray(wave_seeds(lon_total, devices, slots))
-    flipped, spec = call(
-        bind(first_body, lat_rows, devices, slots), (grid_shape, spec_shape), field, seed, far=(field, seed),
-        far_out=(0, 1), name="first",
+    spec = call(
+        bind(first_body, lat_rows, devices, slots), spec_shape, field, seed, far=(field, seed),
+        far_out=(0,), name="first",
         scratch=[buffer((rows, lon_total)), buffer(seed.shape), buffer(wave.shape, jnp.bfloat16),
-                 buffer((rows, lon_total)), buffer(spec_shape.shape), pltpu.SemaphoreType.DMA((3 + QUART,))],
+                 buffer(spec_shape.shape), pltpu.SemaphoreType.DMA((2 + QUART,))],
     )
     spec, far = sphere(spec, near, far, True, False, True)
     count = float(members * fields)
@@ -743,7 +746,7 @@
         bind(center_body, count, part_rows), (grid_shape, inverse_shape, spec_shape), arrive(spec), wave, name="center",
     )
     spec = sphere(spec, near, far, False, True, False)
-    spec = call(ratio_body, spec_shape, arrive(spec), flipped, inverse, wave, name="ratio")
+    spec = call(bind(ratio_body, lat_rows), spec_shape, arrive(spec), field, inverse, wave, name="ratio")
     spec = sphere(spec, near, far, False, False, True)
     part_shape = jax.ShapeDtypeStruct(((members + 1) * part_rows, lon_total), jnp.float32)
     keep, send = call(

time: 97.5 us -> 97.4 us (level)
  no operation moved by 1% of the time
where the time goes in v6:
time: 97.4 us; the launch traced here: 97.1 us
  blocking collectives  64.1 us (66%)
  Pallas kernels  19.9 us (20%)
  starting transfers between devices  7.37 us (8%)
  waiting for transfers between devices  5.02 us (5%)
    all_to_all x5, blocking collectives, exchange(): lax.all_to_all(flat, ('lat', 'field'), split_axis=0, concat_axis=0, tiled...  64.1 us
    pallas_call x9, Pallas kernels, call(): pl.pallas_call(body, out_shape=shapes[0] if single else shapes, in_specs=...  19.9 us
    all_to_all x1, starting transfers between devices, exchange(): lax.all_to_all(flat, ('lat', 'field'), split_axis=0, concat_axis=0, tiled...  7.3 us
    all_to_all x1, waiting for transfers between devices, exchange(): lax.all_to_all(flat, ('lat', 'field'), split_axis=0, concat_axis=0, tiled...  3.59 us
  transfers between devices with their start and end apart: 2, of which 2 were waited for; matrix products, arithmetic and copies ran while one was open for 0% of the time, Pallas kernels for 7%

profile of v6, /device:TPU:0, one launch (start us, length us, event | category | flops | bytes accessed | tf_op | source)
XLA Modules:
  0.0 97.1 jit_solution(7659569009590687452)
XLA Ops:
  0.6 2.4 %first.1 = f32[8,4,16,128]{3,2,1,0:T(8,128)} custom-call(f32[64,1024]{1,0:T(8,128)} %bitcast.8, f32[96,256]{1,0:T(8,128)} %constant.8.clone.refs_1_), custom_call_target="tpu_custom_call" | custom-call | tf_op jit(solution)/shard_map/first/pallas_call | solution.py:687
  3.0 7.3 %all-to-all-start = ((f32[32,16,128]{2,1,0:T(8,128)}), f32[32,16,128]{2,1,0:T(8,128)S(1)}, u32[]{:S(2)}, u32[]{:S(2)}) async-start(f32[32,16,128]{2,1,0:T(8,128)} %bitcast.15), calls=%async_computation | async-start | bytes 524288 | tf_op jit(solution)/shard_map/all_to_all | solution.py:700
  10.3 7.0 %legendre.1 = (bf16[2,2912,256]{2,1,0:T(8,128)(2,1)S(1)}, bf16[2,1440,256]{2,1,0:T(8,128)(2,1)}, f32[1,256]{1,0:T(1,128)S(1)}) custom-call(f32[24,256]{1,0:T(8,128)} %constant.6.clone.refs_0_), custom_call_target="tpu_custom_call" | custom-call | flops 40000000 | bytes 16777216 | tf_op jit(solution)/shard_map/legendre/pallas_call | solution.py:687
  17.3 3.6 %all-to-all-done.refs_0_ = f32[32,16,128]{2,1,0:T(8,128)S(1)} async-done(((f32[32,16,128]{2,1,0:T(8,128)}), f32[32,16,128]{2,1,0:T(8,128)S(1)}, u32[]{:S(2)}, u32[]{:S(2)}) %all-to-all-start) | async-done | bytes 262176 | tf_op jit(solution)/shard_map/all_to_all | solution.py:700
  20.9 0.0 copy-start
  20.9 2.5 %sphere.3 = (f32[32,16,128]{2,1,0:T(8,128)S(1)}, bf16[2,1440,256]{2,1,0:T(8,128)(2,1)S(1)}) custom-call(f32[32,16,128]{2,1,0:T(8,128)S(1)} %all-to-all-done.refs_0_, bf16[2,2912,256]{2,1,0:T(8,128)(2,1)S(1)} %get-tuple-element.14.refs_1_, bf16[2,1440,256]{2,1,0:T(8,128)(2,1)} %get-tuple-element.15.refs_2_, f32[1,256]{1,0:T(1,128)S(1)} %get-tuple-element.16.refs_3_), custom_call_target="tpu_custom_call" | custom-call | tf_op jit(solution)/shard_map/sphere/pallas_call | solution.py:687
  23.4 12.8 %all_to_all.30 = f32[32,16,128]{2,1,0:T(8,128)S(1)} all-to-all(f32[32,16,128]{2,1,0:T(8,128)S(1)} %get-tuple-element.17), channel_id=1, replica_groups=mesh['lat'=16,'field'=2] {'lat','field'}, dimensions={0} | all-to-all | bytes 524288 | tf_op jit(solution)/shard_map/all_to_all | solution.py:700
  36.2 0.0 copy-done
  36.2 1.0 %center.1 = (f32[64,1024]{1,0:T(8,128)S(1)}, f32[64,128]{1,0:T(8,128)S(1)}, f32[8,4,16,128]{3,2,1,0:T(8,128)S(1)}) custom-call(f32[8,4,16,128]{3,2,1,0:T(8,128)S(1)} %bitcast.10, bf16[2,4,256,256]{3,2,1,0:T(8,128)(2,1)S(1)} %copy-done), custom_call_target="tpu_custom_call" | custom-call | tf_op jit(solution)/shard_map/center/pallas_call | solution.py:687
  37.3 12.8 %all_to_all.31.refs_0_ = f32[32,16,128]{2,1,0:T(8,128)S(1)} all-to-all(f32[32,16,128]{2,1,0:T(8,128)S(1)} %bitcast.14), channel_id=1, replica_groups=mesh['lat'=16,'field'=2] {'lat','field'}, dimensions={0} | all-to-all | bytes 524288 | tf_op jit(solution)/shard_map/all_to_all | solution.py:700
  50.1 0.0 copy-start.1
  50.1 2.4 %sphere.4 = f32[32,16,128]{2,1,0:T(8,128)S(1)} custom-call(f32[32,16,128]{2,1,0:T(8,128)S(1)} %all_to_all.31.refs_0_, bf16[2,2912,256]{2,1,0:T(8,128)(2,1)S(1)} %get-tuple-element.14.refs_1_, bf16[2,1440,256]{2,1,0:T(8,128)(2,1)S(1)} %get-tuple-element.19.refs_2_, f32[1,256]{1,0:T(1,128)S(1)} %get-tuple-element.16.refs_3_), custom_call_target="tpu_custom_call" | custom-call | tf_op jit(solution)/shard_map/sphere/pallas_call | solution.py:687
  52.5 12.8 %all_to_all.32 = f32[32,16,128]{2,1,0:T(8,128)S(1)} all-to-all(f32[32,16,128]{2,1,0:T(8,128)S(1)} %sphere.4), channel_id=1, replica_groups=mesh['lat'=16,'field'=2] {'lat','field'}, dimensions={0} | all-to-all | bytes 524288 | tf_op jit(solution)/shard_map/all_to_all | solution.py:700
  65.3 0.0 copy-done.1
  65.3 1.0 %ratio.1 = f32[8,4,16,128]{3,2,1,0:T(8,128)S(1)} custom-call(f32[8,4,16,128]{3,2,1,0:T(8,128)S(1)} %bitcast.11, f32[64,1024]{1,0:T(8,128)S(1)} %bitcast.9, f32[64,128]{1,0:T(8,128)S(1)} %get-tuple-element.20.refs_2_, bf16[2,4,256,256]{3,2,1,0:T(8,128)(2,1)S(1)} %copy-done), custom_call_target="tpu_custom_call" | custom-call | tf_op jit(solution)/shard_map/ratio/pallas_call | solution.py:687
  66.3 12.8 %all_to_all.33.refs_0_ = f32[32,16,128]{2,1,0:T(8,128)S(1)} all-to-all(f32[32,16,128]{2,1,0:T(8,128)S(1)} %bitcast.12), channel_id=1, replica_groups=mesh['lat'=16,'field'=2] {'lat','field'}, dimensions={0} | all-to-all | bytes 524288 | tf_op jit(solution)/shard_map/all_to_all | solution.py:700
  79.1 2.3 %sphere.5 = f32[32,16,128]{2,1,0:T(8,128)S(1)} custom-call(f32[32,16,128]{2,1,0:T(8,128)S(1)} %all_to_all.33.refs_0_, bf16[2,2912,256]{2,1,0:T(8,128)(2,1)S(1)} %get-tuple-element.14.refs_1_, bf16[2,1440,256]{2,1,0:T(8,128)(2,1)S(1)} %get-tuple-element.19.refs_2_, f32[1,256]{1,0:T(1,128)S(1)} %get-tuple-element.16.refs_3_), custom_call_target="tpu_custom_call" | custom-call | tf_op jit(solution)/shard_map/sphere/pallas_call | solution.py:687
  81.4 12.8 %all_to_all.34 = f32[32,16,128]{2,1,0:T(8,128)S(1)} all-to-all(f32[32,16,128]{2,1,0:T(8,128)S(1)} %sphere.5), channel_id=1, replica_groups=mesh['lat'=16,'field'=2] {'lat','field'}, dimensions={0} | all-to-all | bytes 524288 | tf_op jit(solution)/shard_map/all_to_all | solution.py:700
  94.2 0.5 last.1
  94.8 0.1 collective-permute-start
  94.8 1.4 %collective-permute-done.refs_1_ = f32[48,1024]{1,0:T(8,128)S(1)} collective-permute-done((f32[48,1024]{1,0:T(8,128)S(1)}, f32[48,1024]{1,0:T(8,128)S(1)}, u32[]{:S(2)}, u32[]{:S(2)}) %collective-permute-start) | collective-permute-done | bytes 196640 | tf_op jit(solution)/shard_map/ppermute | solution.py:755
  96.3 0.8 final.1
Async XLA Ops:
  3.0 17.9 %all-to-all-start = ((f32[32,16,128]{2,1,0:T(8,128)}), f32[32,16,128]{2,1,0:T(8,128)S(1)}, u32[]{:S(2)}, u32[]{:S(2)}) async-start(f32[32,16,128]{2,1,0:T(8,128)} %bitcast.15), calls=%async_computation | async-start | bytes 524288 | tf_op jit(solution)/shard_map/all_to_all | solution.py:700
  20.9 15.3 %copy-start = (bf16[2,4,256,256]{3,2,1,0:T(8,128)(2,1)S(1)}, bf16[2,4,256,256]{3,2,1,0:T(8,128)(2,1)}, u32[]{:S(2)}) copy-start(bf16[2,4,256,256]{3,2,1,0:T(8,128)(2,1)} %constant.7.clone.refs_1_.refs_3_.refs_2_) | copy-start | bytes 3145732
  50.1 15.2 %copy-start.1 = (f32[2,32,1024]{2,1,0:T(8,128)S(1)}, f32[2,32,1024]{2,1,0:T(8,128)}, u32[]{:S(2)}) copy-start(f32[2,32,1024]{2,1,0:T(8,128)} %param.4) | copy-start | bytes 786436
  94.8 1.5 %collective-permute-start = (f32[48,1024]{1,0:T(8,128)S(1)}, f32[48,1024]{1,0:T(8,128)S(1)}, u32[]{:S(2)}, u32[]{:S(2)}) collective-permute-start(f32[48,1024]{1,0:T(8,128)S(1)} %get-tuple-element.23), channel_id=1, source_target_pairs={{0,1},{1,0},{2,3},{3,2},{4,5},{5,4},{6,7},{7,6},{8,9},{9,8},{10,11... | collective-permute-start | bytes 589832 | tf_op jit(solution)/shard_map/ppermute | solution.py:755

commit v7 on v5

--- a/solution.py
+++ b/solution.py
@@ -407,7 +407,7 @@
     return start + parity * table_rows(degrees, devices, slot)
 
 
-FAR_SLOTS = 3
+FAR_SLOTS = 2
 
 
 def table_part(degrees, devices, slot, parity, near_ref, far_ref):

time: 97.5 us -> 98.7 us (1.012)
  Pallas kernels: 20 us -> 21 us
    pallas_call x9, Pallas kernels: 20 us -> 21 us  [call(): pl.pallas_call(body, out_shape=shapes[0] if single else shapes, in_specs=...]
where the time goes in v7:
time: 98.7 us; the launch traced here: 98.3 us
  blocking collectives  64.1 us (65%)
  Pallas kernels  21 us (21%)
  starting transfers between devices  7.5 us (8%)
  waiting for transfers between devices  5.05 us (5%)
    all_to_all x5, blocking collectives, exchange(): lax.all_to_all(flat, ('lat', 'field'), split_axis=0, concat_axis=0, tiled...  64.1 us
    pallas_call x9, Pallas kernels, call(): pl.pallas_call(body, out_shape=shapes[0] if single else shapes, in_specs=...  21 us
    all_to_all x1, starting transfers between devices, exchange(): lax.all_to_all(flat, ('lat', 'field'), split_axis=0, concat_axis=0, tiled...  7.43 us
    all_to_all x1, waiting for transfers between devices, exchange(): lax.all_to_all(flat, ('lat', 'field'), split_axis=0, concat_axis=0, tiled...  3.62 us
  transfers between devices with their start and end apart: 2, of which 2 were waited for; matrix products, arithmetic and copies ran while one was open for 0% of the time, Pallas kernels for 7%

profile of v7, /device:TPU:0, one launch (start us, length us, event | category | flops | bytes accessed | tf_op | source)
XLA Modules:
  0.0 98.3 jit_solution(11100721490500189867)
XLA Ops:
  0.6 2.4 %first.1 = (f32[64,1024]{1,0:T(8,128)}, f32[8,4,16,128]{3,2,1,0:T(8,128)}) custom-call(f32[64,1024]{1,0:T(8,128)} %bitcast.13, f32[96,256]{1,0:T(8,128)} %constant.8.clone.refs_1_), custom_call_target="tpu_custom_call" | custom-call | tf_op jit(solution)/shard_map/first/pallas_call | solution.py:684
  3.0 7.4 %all-to-all-start = ((f32[32,16,128]{2,1,0:T(8,128)}), f32[32,16,128]{2,1,0:T(8,128)}, u32[]{:S(2)}, u32[]{:S(2)}) async-start(f32[32,16,128]{2,1,0:T(8,128)} %bitcast.14), calls=%async_computation | async-start | bytes 524288 | tf_op jit(solution)/shard_map/all_to_all | solution.py:697
  10.5 6.9 %legendre.1 = (bf16[2,3360,256]{2,1,0:T(8,128)(2,1)S(1)}, bf16[2,992,256]{2,1,0:T(8,128)(2,1)}, f32[1,256]{1,0:T(1,128)S(1)}) custom-call(f32[24,256]{1,0:T(8,128)} %constant.6.clone.refs_0_), custom_call_target="tpu_custom_call" | custom-call | flops 40000000 | bytes 16777216 | tf_op jit(solution)/shard_map/legendre/pallas_call | solution.py:684
  17.4 3.6 %all-to-all-done.refs_0_ = f32[32,16,128]{2,1,0:T(8,128)} async-done(((f32[32,16,128]{2,1,0:T(8,128)}), f32[32,16,128]{2,1,0:T(8,128)}, u32[]{:S(2)}, u32[]{:S(2)}) %all-to-all-start) | async-done | bytes 262176 | tf_op jit(solution)/shard_map/all_to_all | solution.py:697
  21.1 0.0 copy-start
  21.1 3.6 %sphere.3 = (f32[32,16,128]{2,1,0:T(8,128)S(1)}, bf16[2,992,256]{2,1,0:T(8,128)(2,1)S(1)}) custom-call(f32[32,16,128]{2,1,0:T(8,128)} %all-to-all-done.refs_0_, bf16[2,3360,256]{2,1,0:T(8,128)(2,1)S(1)} %get-tuple-element.17.refs_1_, bf16[2,992,256]{2,1,0:T(8,128)(2,1)} %get-tuple-element.18.refs_2_, f32[1,256]{1,0:T(1,128)S(1)} %get-tuple-element.19.refs_3_), custom_call_target="tpu_custom_call" | custom-call | tf_op jit(solution)/shard_map/sphere/pallas_call | solution.py:684
  24.7 12.8 %all_to_all.30 = f32[32,16,128]{2,1,0:T(8,128)S(1)} all-to-all(f32[32,16,128]{2,1,0:T(8,128)S(1)} %get-tuple-element.20), channel_id=1, replica_groups=mesh['lat'=16,'field'=2] {'lat','field'}, dimensions={0} | all-to-all | bytes 524288 | tf_op jit(solution)/shard_map/all_to_all | solution.py:697
  37.5 0.0 copy-done
  37.5 0.0 copy-start.1
  37.5 1.0 %center.1 = (f32[64,1024]{1,0:T(8,128)S(1)}, f32[64,128]{1,0:T(8,128)S(1)}, f32[8,4,16,128]{3,2,1,0:T(8,128)S(1)}) custom-call(f32[8,4,16,128]{3,2,1,0:T(8,128)S(1)} %bitcast.8, bf16[2,4,256,256]{3,2,1,0:T(8,128)(2,1)S(1)} %copy-done), custom_call_target="tpu_custom_call" | custom-call | tf_op jit(solution)/shard_map/center/pallas_call | solution.py:684
  38.5 12.8 %all_to_all.31.refs_0_ = f32[32,16,128]{2,1,0:T(8,128)S(1)} all-to-all(f32[32,16,128]{2,1,0:T(8,128)S(1)} %bitcast.12), channel_id=1, replica_groups=mesh['lat'=16,'field'=2] {'lat','field'}, dimensions={0} | all-to-all | bytes 524288 | tf_op jit(solution)/shard_map/all_to_all | solution.py:697
  51.3 2.4 %sphere.4 = f32[32,16,128]{2,1,0:T(8,128)S(1)} custom-call(f32[32,16,128]{2,1,0:T(8,128)S(1)} %all_to_all.31.refs_0_, bf16[2,3360,256]{2,1,0:T(8,128)(2,1)S(1)} %get-tuple-element.17.refs_1_, bf16[2,992,256]{2,1,0:T(8,128)(2,1)S(1)} %get-tuple-element.22.refs_2_, f32[1,256]{1,0:T(1,128)S(1)} %get-tuple-element.19.refs_3_), custom_call_target="tpu_custom_call" | custom-call | tf_op jit(solution)/shard_map/sphere/pallas_call | solution.py:684
  53.7 12.8 %all_to_all.32 = f32[32,16,128]{2,1,0:T(8,128)S(1)} all-to-all(f32[32,16,128]{2,1,0:T(8,128)S(1)} %sphere.4), channel_id=1, replica_groups=mesh['lat'=16,'field'=2] {'lat','field'}, dimensions={0} | all-to-all | bytes 524288 | tf_op jit(solution)/shard_map/all_to_all | solution.py:697
  66.5 0.0 copy-done.1
  66.5 1.0 ratio.1
  67.5 12.8 %all_to_all.33.refs_0_ = f32[32,16,128]{2,1,0:T(8,128)S(1)} all-to-all(f32[32,16,128]{2,1,0:T(8,128)S(1)} %bitcast.10), channel_id=1, replica_groups=mesh['lat'=16,'field'=2] {'lat','field'}, dimensions={0} | all-to-all | bytes 524288 | tf_op jit(solution)/shard_map/all_to_all | solution.py:697
  80.3 2.4 %sphere.5 = f32[32,16,128]{2,1,0:T(8,128)S(1)} custom-call(f32[32,16,128]{2,1,0:T(8,128)S(1)} %all_to_all.33.refs_0_, bf16[2,3360,256]{2,1,0:T(8,128)(2,1)S(1)} %get-tuple-element.17.refs_1_, bf16[2,992,256]{2,1,0:T(8,128)(2,1)S(1)} %get-tuple-element.22.refs_2_, f32[1,256]{1,0:T(1,128)S(1)} %get-tuple-element.19.refs_3_), custom_call_target="tpu_custom_call" | custom-call | tf_op jit(solution)/shard_map/sphere/pallas_call | solution.py:684
  82.7 12.8 %all_to_all.34 = f32[32,16,128]{2,1,0:T(8,128)S(1)} all-to-all(f32[32,16,128]{2,1,0:T(8,128)S(1)} %sphere.5), channel_id=1, replica_groups=mesh['lat'=16,'field'=2] {'lat','field'}, dimensions={0} | all-to-all | bytes 524288 | tf_op jit(solution)/shard_map/all_to_all | solution.py:697
  95.5 0.5 last.1
  96.0 0.1 collective-permute-start
  96.1 1.4 %collective-permute-done.refs_1_ = f32[48,1024]{1,0:T(8,128)S(1)} collective-permute-done((f32[48,1024]{1,0:T(8,128)S(1)}, f32[48,1024]{1,0:T(8,128)S(1)}, u32[]{:S(2)}, u32[]{:S(2)}) %collective-permute-start) | collective-permute-done | bytes 196640 | tf_op jit(solution)/shard_map/ppermute | solution.py:752
  97.5 0.8 final.1
Async XLA Ops:
  3.0 18.0 %all-to-all-start = ((f32[32,16,128]{2,1,0:T(8,128)}), f32[32,16,128]{2,1,0:T(8,128)}, u32[]{:S(2)}, u32[]{:S(2)}) async-start(f32[32,16,128]{2,1,0:T(8,128)} %bitcast.14), calls=%async_computation | async-start | bytes 524288 | tf_op jit(solution)/shard_map/all_to_all | solution.py:697
  21.1 16.4 %copy-start = (bf16[2,4,256,256]{3,2,1,0:T(8,128)(2,1)S(1)}, bf16[2,4,256,256]{3,2,1,0:T(8,128)(2,1)}, u32[]{:S(2)}) copy-start(bf16[2,4,256,256]{3,2,1,0:T(8,128)(2,1)} %constant.7.clone.refs_1_.wave_ref.refs_2_) | copy-start | bytes 3145732
  37.5 29.1 %copy-start.1 = (f32[64,1024]{1,0:T(8,128)S(1)}, f32[64,1024]{1,0:T(8,128)}, u32[]{:S(2)}) copy-start(f32[64,1024]{1,0:T(8,128)} %get-tuple-element.23.field_ref) | copy-start | bytes 786436
  96.0 1.5 %collective-permute-start = (f32[48,1024]{1,0:T(8,128)S(1)}, f32[48,1024]{1,0:T(8,128)S(1)}, u32[]{:S(2)}, u32[]{:S(2)}) collective-permute-start(f32[48,1024]{1,0:T(8,128)S(1)} %get-tuple-element.27), channel_id=1, source_target_pairs={{0,1},{1,0},{2,3},{3,2},{4,5},{5,4},{6,7},{7,6},{8,9},{9,8},{10,11... | collective-permute-start | bytes 589832 | tf_op jit(solution)/shard_map/ppermute | solution.py:752
